TPU v7x, 512 devices: a whole 4x4x16 slice. The times are simulated.
512 devices in a mesh: seq: 64 (over y, z), section: 8 (over x, core).
Axes of the slice: x: 4, y: 4, z: 16, core: 2. Of those that a mesh axis runs over, the one named last changes fastest.
Arguments:
- query_rows: bfloat16 [32768, 4096], P('seq', 'section'), may hold values from -6 to 6
- key_rows: bfloat16 [32768, 4096], P('seq', 'section'), may hold values from -6 to 6
- value_rows: bfloat16 [32768, 4096], P('seq', 'section'), may hold values from -6 to 6
- log_decay: float32 [32768, 32], P('seq', 'section'), may hold values from -1 to 0
- lengths: int32 [32], replicated, may hold values from 1 to 16384, as said below
- norm_gain: float32 [4096], P('section'), may hold values from 0.1 to 1.9
Outputs:
- next_input: bfloat16 [32768, 4096], P(('seq', 'section'))
Inputs may be any that keep to these rules, and one draw needn't show every extreme that they name: The lengths of 32 documents in order, summing to 32768; the document at index (31) // 2 is the longest, exactly 16384 tokens, and starts at token 8192.
All inputs are finite; a program needn't handle non-finite values.
Results may differ from a plain program's by a relative error of at most 0.0058.
Values may be sent and summed in bfloat16 or wider, within the bound.
No kernel may reach another device: no remote copies, remote signals or barrier semaphores. Data moves between devices by JAX's collectives and lax.ppermute only.
A program may use at most 64 MiB of HBM per device.

v0:
```python
import math

import jax
import jax.numpy as jnp
from jax import lax
from jax.sharding import PartitionSpec as P


def entering(value, axis, join, neutral):
    count, mine = (lax.axis_size(axis), lax.axis_index(axis))
    pieces = jax.tree.map(lambda part: lax.all_gather(part, axis), value)
    running = jax.tree.map(
        lambda part, zero: jnp.full_like(part, 0) + jnp.asarray(zero, part.dtype), value, neutral
    )

    def hop(position, running):
        longer = join(running, jax.tree.map(lambda part: part[position], pieces))
        return jax.tree.map(lambda new, old: jnp.where(position < mine, new, old), longer, running)

    return lax.fori_loop(0, count - 1, hop, running)


def head_within(items):
    query_head, key_head, value_head, cumul_head, allowed, scale_factor = items
    scores = jnp.dot(query_head, key_head.T, preferred_element_type=jnp.float32)
    log_gap = cumul_head[:, None] - cumul_head[None, :]
    safe_gap = jnp.where(allowed, log_gap, 0.0)
    weights = jnp.where(allowed, scores * scale_factor * jnp.exp(safe_gap), 0.0).astype(
        jnp.bfloat16
    )
    return jnp.dot(weights, value_head, preferred_element_type=jnp.float32)


def block_terms(queries, key_block, value_block, decay_block, doc_ids, prev_doc):
    tok_rows = queries.shape[0]
    head_size = queries.shape[2]
    scale_factor = 1.0 / math.sqrt(head_size)
    cumulative = jnp.cumsum(decay_block, axis=0)
    position = jnp.arange(tok_rows, dtype=jnp.int32)
    allowed = (position[:, None] >= position[None, :]) & (doc_ids[:, None] == doc_ids[None, :])

    def per_head(items):
        return head_within((items[0], items[1], items[2], items[3], allowed, scale_factor))

    within_heads = lax.map(
        per_head,
        (
            queries.transpose(1, 0, 2),
            key_block.transpose(1, 0, 2),
            value_block.transpose(1, 0, 2),
            cumulative.T,
        ),
    )
    within = within_heads.transpose(1, 0, 2)
    end_log = cumulative[-1]
    in_last = (doc_ids == doc_ids[-1]).astype(jnp.float32)
    key_scale = jnp.exp(end_log[None, :] - cumulative) * in_last[:, None]
    decayed_keys = (key_block.astype(jnp.float32) * key_scale[:, :, None]).astype(jnp.bfloat16)
    block_state = jnp.einsum(
        "thd,the->hde", decayed_keys, value_block, preferred_element_type=jnp.float32
    )
    opened = (doc_ids[-1] != prev_doc).astype(jnp.float32)
    decayed_queries = (
        queries.astype(jnp.float32) * (jnp.exp(cumulative) * scale_factor)[:, :, None]
    ).astype(jnp.bfloat16)
    carried = (doc_ids == prev_doc).astype(jnp.float32)
    return (within, decayed_queries, carried, end_log, opened, block_state)


def finish(within, decayed_queries, carried, incoming, gain_heads):
    incoming_low = incoming.astype(jnp.bfloat16)
    carried_out = jnp.einsum(
        "thd,hde->the", decayed_queries, incoming_low, preferred_element_type=jnp.float32
    )
    attention = within + carried[:, None, None] * carried_out
    mean_square = jnp.mean(attention * attention, axis=-1, keepdims=True)
    normed = attention * lax.rsqrt(mean_square + 1e-05) * gain_heads[None]
    return normed.astype(jnp.bfloat16)


def combine(earlier, later):
    kept = (1.0 - later[1]) * jnp.exp(later[0])
    return (
        earlier[0] + later[0],
        jnp.maximum(earlier[1], later[1]),
        later[2] + kept[:, None, None] * earlier[2],
    )


def shards(query_rows, key_rows, value_rows, log_decay, lengths, norm_gain):
    tok_rows = query_rows.shape[0]
    feature_width = query_rows.shape[1]
    heads = log_decay.shape[1]
    head_size = feature_width // heads
    queries = query_rows.reshape(tok_rows, heads, head_size)
    key_block = key_rows.reshape(tok_rows, heads, head_size)
    value_block = value_rows.reshape(tok_rows, heads, head_size)
    doc_ends = jnp.cumsum(lengths)
    first_row = lax.axis_index("seq") * tok_rows
    positions = first_row + jnp.arange(tok_rows, dtype=jnp.int32)
    doc_ids = jnp.sum((doc_ends[None, :] <= positions[:, None]).astype(jnp.int32), axis=1)
    prev_doc = jnp.sum((doc_ends <= first_row - 1).astype(jnp.int32))
    within, decayed_queries, carried, end_log, opened, block_state = block_terms(
        queries, key_block, value_block, log_decay, doc_ids, prev_doc
    )
    identity = (
        jnp.zeros((heads,), jnp.float32),
        jnp.zeros((), jnp.float32),
        jnp.zeros((heads, head_size, head_size), jnp.float32),
    )
    scanned = entering((end_log, opened, block_state), "seq", combine, identity)
    incoming = scanned[2]
    gain_heads = norm_gain.reshape(heads, head_size)
    normed = finish(within, decayed_queries, carried, incoming, gain_heads)
    return lax.all_to_all(
        normed.reshape(tok_rows, feature_width), "section", split_axis=0, concat_axis=1, tiled=True
    )


def solution(mesh):
    placed = (
        P("seq", "section"),
        P("seq", "section"),
        P("seq", "section"),
        P("seq", "section"),
        P(),
        P("section"),
    )
    return jax.shard_map(
        shards, mesh=mesh, in_specs=placed, out_specs=P(("seq", "section"), None), check_vma=False
    )
```

profile of v0, /device:TPU:8, one launch (start us, length us, event | category | flops | bytes accessed | tf_op | source)
XLA Modules:
  0.0 415.5 jit_solution(9530744983872537273)
XLA Ops:
  9.6 1.2 reduce-window.18
  11.4 1.3 copy.51
  12.7 1.3 copy.52
  13.9 1.3 compare_convert_fusion
  17.7 1.3 copy.50
  18.9 1.3 dynamic-slice
  21.0 129.1 %all-reduce = f32[64]{0:T(128)S(1)} all-reduce(f32[64]{0:T(128)S(1)} %dynamic-update-slice), channel_id=1, replica_groups=mesh['seq'=64,'section'=8] {'seq'}, use_global_device_ids=true, to_apply=%add | all-reduce | flops 64 | bytes 512
  150.1 92.2 %all-gather.1 = f32[64,1,4]{2,1,0:T(1,128)S(1)} all-gather(f32[1,1,4]{2,1,0:T(1,128)S(1)} %bitcast.102), channel_id=1, replica_groups=mesh['seq'=64,'section'=8] {'seq'}, dimensions={0}, use_global_device_ids=true | all-gather | bytes 1040 | tf_op jit(solution)/shard_map/all_gather | solution.py:11
  242.3 2.7 while.25
  245.1 147.2 %while.26 = (s32[]{:T(128)}, f32[4,128,128]{2,1,0:T(8,128)S(1)}, s32[]{:T(128)}, f32[64,4,128,128]{3,2,1,0:T(8,128)}, f32[64]{0:T(128)S(1)}, /*index=5*/f32[64,4]{1,0:T(8,128)S(1)}, s32[]{:T(128)}, f32[1]{0:T(128)}, s32[]{:T(128)}) while((s32[]{:T(128)}, f32[4,128,128]{2,1,0:T(8,128)S(1)}, s32[]{:T(128)}, ...), condition=%wide.region_8.9_spmd.clone, body=%wide.region_7.8_spmd.clone.sunk | while | flops 262153 | bytes 786629 | solution.py:20
  246.3 1.1 fusion.53
  248.7 1.1 fusion.53
  251.0 1.1 fusion.53
  253.3 1.1 fusion.53
  255.7 1.1 fusion.53
  258.0 1.1 fusion.53
  260.4 1.1 fusion.53
  262.7 1.1 fusion.53
  265.0 1.1 fusion.53
  267.4 1.1 fusion.53
  269.7 1.1 fusion.53
  272.0 1.1 fusion.53
  274.4 1.1 fusion.53
  276.7 1.1 fusion.53
  279.0 1.1 fusion.53
  281.4 1.1 fusion.53
  283.7 1.1 fusion.53
  286.1 1.1 fusion.53
  288.4 1.1 fusion.53
  290.7 1.1 fusion.53
  293.1 1.1 fusion.53
  295.4 1.1 fusion.53
  297.7 1.1 fusion.53
  300.1 1.1 fusion.53
  302.4 1.1 fusion.53
  304.8 1.1 fusion.53
  307.1 1.1 fusion.53
  309.4 1.1 fusion.53
  311.8 1.1 fusion.53
  314.1 1.1 fusion.53
  316.4 1.1 fusion.53
  318.8 1.1 fusion.53
  321.1 1.1 fusion.53
  323.4 1.1 fusion.53
  325.8 1.1 fusion.53
  328.1 1.1 fusion.53
  330.5 1.1 fusion.53
  332.8 1.1 fusion.53
  335.1 1.1 fusion.53
  337.5 1.1 fusion.53
  344.5 1.1 fusion.53
  346.8 1.1 fusion.53
  349.2 1.1 fusion.53
  351.5 1.1 fusion.53
  353.8 1.1 fusion.53
  356.2 1.1 fusion.53
  367.8 1.1 fusion.53
  370.2 1.1 fusion.53
  372.5 1.1 fusion.53
  374.9 1.1 fusion.53
  377.2 1.1 fusion.53
  388.9 1.1 fusion.53
  391.2 1.1 fusion.53
  393.4 14.5 %all_to_all.19 = bf16[8,64,512]{2,1,0:T(8,128)(2,1)S(1)} all-to-all(bf16[8,64,512]{2,1,0:T(8,128)(2,1)S(1)} %all_to_all.14), channel_id=1, replica_groups=mesh['seq'=64,'section'=8] {'section'}, dimensions={0} | all-to-all | bytes 1048576 | tf_op jit(solution)/shard_map/all_to_all | solution.py:115
  (174 shorter events, 58.4 us)
Async XLA Ops:
  6.5 386.2 %copy-start = (f32[512]{0:T(512)S(1)}, f32[512]{0:T(512)}, u32[]{:S(2)}) copy-start(f32[512]{0:T(512)} %param.15) | copy-start | bytes 6148
  6.5 238.5 %all-gather.4.cloned.1.call-start = ((), (), s32[]{:S(2)}) async-start(), calls=%async_computation.1 | async-start | bytes 17039360 | tf_op jit(solution)/shard_map/all_gather | solution.py:11
Sparse Core Ops, SparseCore 0:
  16.5 197.6 all-gather.3
where the time goes:
time: 419 us; the launch traced here: 416 us
  blocking collectives  236 us (56%)
  other arithmetic  71.2 us (17%)
  local copies, waits for them, and re-layouts  46.6 us (11%)
  loops' own time  43.1 us (10%)
  between operations  14.8 us (4%)
    unnamed x1, blocking collectives  129 us
    all_gather x1, blocking collectives, entering(): pieces = jax.tree.map(lambda part: lax.all_gather(part, axis), value)  92.2 us
    select_n x63, other arithmetic, hop(): jnp.where(position < mine, new, old)  66.3 us
    another operation x1, loops' own time, entering(): return lax.fori_loop(0, count - 1, hop, running)  43 us
    dynamic_slice x63, local copies, waits for them, and re-layouts, hop(): longer = join(running, jax.tree.map(lambda part: part[position], pieces))  36.9 us
    all_to_all x1, blocking collectives, shards(): lax.all_to_all(normed.reshape(tok_rows, feature_width), 'section', split_...  14.5 us
  transfers between devices with their start and end apart: 1, of which 0 were waited for; matrix products, arithmetic and copies ran while one was open for 1% of the time, Pallas kernels for 0%

commit v1 on v0

v1 whole, which is shorter than its diff:
```python
import math

import jax
import jax.numpy as jnp
from jax import lax
from jax.experimental import pallas as pl
from jax.experimental.pallas import tpu as pltpu
from jax.sharding import PartitionSpec as P

F32, BF16 = jnp.float32, jnp.bfloat16
NEVER = -1e30
DECAY_ROWS = 8


def dot(a, b, contract):
    return lax.dot_general(a, b, ((contract[:1], contract[1:]), ((), ())), preferred_element_type=F32)


def three_parts(x):
    high = x.astype(BF16)
    rest = x - high.astype(F32)
    mid = rest.astype(BF16)
    return high, mid, (rest - mid.astype(F32)).astype(BF16)


def document_limits(lengths_ref, first_row, rows):
    last = first_row + rows - 1
    start_last, end_prev, begin = jnp.int32(0), jnp.int32(0), jnp.int32(0)
    found = jnp.bool_(False)
    for doc in range(lengths_ref.shape[0]):
        start_last = jnp.where(begin <= last, begin, start_last)
        end = begin + lengths_ref[doc]
        end_prev = jnp.where(found, end_prev, end)
        found = jnp.logical_or(found, end >= first_row)
        begin = end
    return start_last, end_prev


def state_kernel(lengths_ref, key_ref, value_ref, decay_ref, out_ref):
    rows, heads = decay_ref.shape
    dim = key_ref.shape[1] // heads
    holders, slots = out_ref.shape[0], heads * dim // out_ref.shape[0]
    first_row = lax.axis_index("seq") * rows
    start_last, _ = document_limits(lengths_ref, first_row, rows)
    row = lax.broadcasted_iota(jnp.int32, (rows, rows), 0)
    col = lax.broadcasted_iota(jnp.int32, (rows, rows), 1)
    later = (col > row).astype(F32).astype(BF16)
    decay = decay_ref[...]
    to_end = sum(dot(later, part, (1, 0)) for part in three_parts(decay))
    position = first_row + lax.broadcasted_iota(jnp.int32, (rows, 1), 0)
    in_last = position >= start_last
    key_scale = jnp.where(in_last, jnp.exp(to_end), 0.0)
    end_log = to_end[0:1, :] + decay[0:1, :]
    end_log = jnp.where(start_last >= first_row, NEVER, end_log)
    lines = lax.broadcasted_iota(jnp.int32, (DECAY_ROWS, dim), 0)
    per_head = holders // heads
    for head in range(heads):
        span = pl.ds(head * dim, dim)
        keys = (key_ref[:, span].astype(F32) * key_scale[:, head : head + 1]).astype(BF16)
        state = dot(keys, value_ref[:, span], (0, 0)).astype(BF16)
        high, mid, low = (p.astype(F32) for p in three_parts(end_log[:, head : head + 1]))
        sent = jnp.where(lines == 0, high, jnp.where(lines == 1, mid, jnp.where(lines == 2, low, 0.0)))
        sent = sent.astype(BF16)
        for i in range(per_head):
            out_ref[head * per_head + i, 0:slots, :] = state[i * slots : (i + 1) * slots, :]
            out_ref[head * per_head + i, slots : slots + DECAY_ROWS, :] = sent


def within_kernel(lengths_ref, query_ref, key_ref, value_ref, decay_ref, within_ref, decayed_ref):
    rows, heads = decay_ref.shape
    dim = key_ref.shape[1] // heads
    scale = 1.0 / math.sqrt(dim)
    step = 128
    first_row = lax.axis_index("seq") * rows
    _, end_prev = document_limits(lengths_ref, first_row, rows)
    row = lax.broadcasted_iota(jnp.int32, (rows, rows), 0)
    col = lax.broadcasted_iota(jnp.int32, (rows, rows), 1)
    upto = (col <= row).astype(F32).astype(BF16)
    parts = three_parts(decay_ref[...])
    cumul_col = sum(dot(upto, part, (1, 0)) for part in parts)
    cumul_row = sum(dot(part, upto, (0, 1)) for part in parts)
    spot_row = first_row + lax.broadcasted_iota(jnp.int32, (1, rows), 1)
    lane = lax.broadcasted_iota(jnp.int32, (1, dim), 1)
    doc_row = jnp.zeros((1, rows), F32)
    ends = jnp.zeros((1, dim), jnp.int32)
    end = jnp.int32(0)
    for doc in range(lengths_ref.shape[0]):
        end = end + lengths_ref[doc]
        doc_row = doc_row + jnp.where(spot_row >= end, 1.0, 0.0)
        ends = ends + jnp.where(lane >= doc, lengths_ref[doc], 0)
    position = first_row + lax.broadcasted_iota(jnp.int32, (rows, 1), 0)
    doc_col = jnp.sum(jnp.where(ends <= position, 1.0, 0.0), axis=1, keepdims=True)
    query_scale = jnp.where(position < end_prev, jnp.exp(cumul_col) * scale, 0.0)
    for head in range(heads):
        span = pl.ds(head * dim, dim)
        decayed_ref[:, span] = (query_ref[:, span].astype(F32) * query_scale[:, head : head + 1]).astype(BF16)
    for at in range(0, rows, step):
        upper = at + step
        t = at + lax.broadcasted_iota(jnp.int32, (step, upper), 0)
        u = lax.broadcasted_iota(jnp.int32, (step, upper), 1)
        allowed = jnp.logical_and(u <= t, doc_col[at:upper] == doc_row[:, :upper])
        shut = jnp.where(allowed, 0.0, NEVER)
        for head in range(heads):
            span = pl.ds(head * dim, dim)
            scores = dot(query_ref[pl.ds(at, step), span], key_ref[pl.ds(0, upper), span], (1, 1))
            gap = cumul_col[at:upper, head : head + 1] - cumul_row[head : head + 1, :upper]
            weights = jnp.where(allowed, scores * scale * jnp.exp(jnp.minimum(gap, 0.0) + shut), 0.0).astype(BF16)
            within_ref[pl.ds(at, step), span] = dot(weights, value_ref[pl.ds(0, upper), span], (1, 0))


def scan_kernel(taken_ref, out_ref):
    blocks, slots, dim = out_ref.shape
    carry = jnp.zeros((slots, dim), F32)
    for block in range(blocks):
        out_ref[block] = carry.astype(BF16)
        tail = taken_ref[block, slots : slots + DECAY_ROWS, :].astype(F32)
        kept = jnp.exp(tail[0:1] + tail[1:2] + tail[2:3])
        carry = taken_ref[block, 0:slots, :].astype(F32) + kept * carry


def finish_kernel(within_ref, decayed_ref, incoming_ref, gain_ref, out_ref):
    dim = incoming_ref.shape[1]
    for head in range(incoming_ref.shape[0] // dim):
        span = pl.ds(head * dim, dim)
        carried = dot(decayed_ref[:, span], incoming_ref[span, :], (1, 0))
        attention = within_ref[:, span] + carried
        mean_square = jnp.mean(attention * attention, axis=1, keepdims=True)
        out_ref[:, span] = (attention * lax.rsqrt(mean_square + 1e-05) * gain_ref[:, span]).astype(BF16)


def params():
    return pltpu.CompilerParams(vmem_limit_bytes=32 << 20)


def shards(query_rows, key_rows, value_rows, log_decay, lengths, norm_gain):
    rows, width = query_rows.shape
    heads = log_decay.shape[1]
    dim = width // heads
    blocks = lax.axis_size("seq")
    quarter = blocks // 4
    middle = list(range(quarter, 3 * quarter))
    chains = [middle, [b for b in range(blocks) if b not in middle]]
    holders = len(middle)
    slots = width // holders
    smem = pl.BlockSpec(memory_space=pltpu.SMEM)
    vmem = pl.BlockSpec(memory_space=pltpu.VMEM)

    states = pl.pallas_call(
        state_kernel,
        out_shape=jax.ShapeDtypeStruct((holders, slots + DECAY_ROWS, dim), BF16),
        in_specs=[smem, vmem, vmem, vmem],
        out_specs=vmem,
        compiler_params=params(),
        name="states",
    )(lengths, key_rows, value_rows, log_decay)
    taken = lax.all_to_all(states, "seq", split_axis=0, concat_axis=0, tiled=True, axis_index_groups=chains)
    within, decayed = pl.pallas_call(
        within_kernel,
        out_shape=(jax.ShapeDtypeStruct((rows, width), F32), jax.ShapeDtypeStruct((rows, width), BF16)),
        in_specs=[smem, vmem, vmem, vmem, vmem],
        out_specs=(vmem, vmem),
        compiler_params=params(),
        cost_estimate=pl.CostEstimate(
            flops=4 * rows * rows * width, bytes_accessed=9 * rows * width, transcendentals=rows * rows * heads
        ),
        name="within",
    )(lengths, query_rows, key_rows, value_rows, log_decay)
    given = pl.pallas_call(
        scan_kernel,
        out_shape=jax.ShapeDtypeStruct((holders, slots, dim), BF16),
        in_specs=[vmem],
        out_specs=vmem,
        compiler_params=params(),
        name="scan",
    )(taken)
    incoming = lax.all_to_all(given, "seq", split_axis=0, concat_axis=0, tiled=True, axis_index_groups=chains)
    step = rows // 4
    normed = pl.pallas_call(
        finish_kernel,
        out_shape=jax.ShapeDtypeStruct((rows, width), BF16),
        grid=(rows // step,),
        in_specs=[
            pl.BlockSpec((step, width), lambda i: (i, 0)),
            pl.BlockSpec((step, width), lambda i: (i, 0)),
            pl.BlockSpec((width, dim), lambda i: (0, 0)),
            pl.BlockSpec((1, width), lambda i: (0, 0)),
        ],
        out_specs=pl.BlockSpec((step, width), lambda i: (i, 0)),
        compiler_params=params(),
        name="finish",
    )(within, decayed, incoming.reshape(width, dim), norm_gain.reshape(1, width))
    return lax.all_to_all(normed, "section", split_axis=0, concat_axis=1, tiled=True)


def solution(mesh):
    placed = (
        P("seq", "section"),
        P("seq", "section"),
        P("seq", "section"),
        P("seq", "section"),
        P(),
        P("section"),
    )
    return jax.shard_map(
        shards, mesh=mesh, in_specs=placed, out_specs=P(("seq", "section"), None), check_vma=False
    )
```

time: 419 us -> 83.1 us (0.20)
  the two profiles are of different devices: /device:TPU:8 before, /device:TPU:1 now
where the time goes in v1:
time: 83.1 us; the launch traced here: 82.7 us
  blocking collectives  53.7 us (65%)
  waiting for transfers between devices  11.9 us (14%)
  Pallas kernels  7.52 us (9%)
  starting transfers between devices  5.01 us (6%)
  local copies, waits for them, and re-layouts  4.46 us (5%)
    all_to_all x1, blocking collectives, shards(): lax.all_to_all(states, 'seq', split_axis=0, concat_axis=0, tiled=True, ax...  36.8 us
    all_to_all x1, blocking collectives, shards(): lax.all_to_all(normed, 'section', split_axis=0, concat_axis=1, tiled=True)  16.9 us
    all_to_all x1, waiting for transfers between devices, shards(): lax.all_to_all(given, 'seq', split_axis=0, concat_axis=0, tiled=True, axi...  11.9 us
    all_to_all x1, starting transfers between devices, shards(): lax.all_to_all(given, 'seq', split_axis=0, concat_axis=0, tiled=True, axi...  5.01 us
    pallas_call x1, Pallas kernels, shards(): pl.pallas_call(within_kernel, out_shape=(jax.ShapeDtypeStruct((rows, widt...  3.7 us
    unnamed x15, local copies, waits for them, and re-layouts  3.62 us
    pallas_call x1, Pallas kernels, shards(): pl.pallas_call(state_kernel, out_shape=jax.ShapeDtypeStruct((holders, slo...  1.88 us
  transfers between devices with their start and end apart: 1, of which 1 were waited for; matrix products, arithmetic and copies ran while one was open for 0% of the time, Pallas kernels for 4%

profile of v1, /device:TPU:1, one launch (start us, length us, event | category | flops | bytes accessed | tf_op | source)
XLA Modules:
  0.0 82.7 jit_solution(16222106011876238959)
XLA Ops:
  0.0 0.0 copy-start.5
  0.0 0.8 %copy.7.decay_ref = f32[512,4]{1,0:T(8,128)S(1)} copy(f32[512,4]{0,1:T(4,128)} %param.9) | data formatting | bytes 16384 | tf_op args[3]
  0.9 0.0 copy-done.5
  0.9 0.0 copy-start
  0.9 1.0 %copy-done = bf16[512,512]{1,0:T(8,128)(2,1)S(1)} copy-done((bf16[512,512]{1,0:T(8,128)(2,1)S(1)}, bf16[512,512]{1,0:T(8,128)(2,1)}, u32[]{:S(2)}) %copy-start) | copy-done | bytes 524312
  1.9 0.0 copy-start.2
  1.9 1.0 %copy-done.2 = bf16[512,512]{1,0:T(8,128)(2,1)S(1)} copy-done((bf16[512,512]{1,0:T(8,128)(2,1)S(1)}, bf16[512,512]{1,0:T(8,128)(2,1)}, u32[]{:S(2)}) %copy-start.2) | copy-done | bytes 524312
  3.0 0.0 copy-start.3
  3.0 0.0 copy-start.6
  3.0 1.9 %states.1 = bf16[32,24,128]{2,1,0:T(8,128)(2,1)S(1)} custom-call(s32[32]{0:T(128)S(1)} %copy-done.5, bf16[512,512]{1,0:T(8,128)(2,1)S(1)} %copy-done, bf16[512,512]{1,0:T(8,128)(2,1)S(1)} %copy-done.2, f32[512,4]{1,0:T(8,128)S(1)} %copy.7.decay_ref), custom_call_target="tpu_custom_call" | custom-call | tf_op jit(solution)/shard_map/states/pallas_call | solution.py:148
  4.8 0.0 copy-start.1
  4.9 36.8 %all_to_all.29.taken_ref = bf16[32,24,128]{2,1,0:T(8,128)(2,1)S(1)} all-to-all(bf16[32,24,128]{2,1,0:T(8,128)(2,1)S(1)} %states.1), channel_id=1, replica_groups={{128,136,144,152,160,168,176,184,192,200,208,216,224,232,240,248,256,26..., dimensions={0} | all-to-all | bytes 393216 | tf_op jit(solution)/shard_map/all_to_all | solution.py:156
  41.6 0.7 scan.1
  42.3 5.0 %all-to-all-start.1 = ((bf16[32,16,128]{2,1,0:T(8,128)(2,1)}), bf16[32,16,128]{2,1,0:T(8,128)(2,1)S(1)}, u32[]{:S(2)}, u32[]{:S(2)}) async-start(bf16[32,16,128]{2,1,0:T(8,128)(2,1)} %scan.1), calls=%async_computation.1 | async-start | bytes 262144 | tf_op jit(solution)/shard_map/all_to_all | solution.py:176
  47.4 0.0 copy-done.3
  47.4 0.0 copy-done.6
  47.4 0.0 copy-done.1
  47.4 3.7 %within.1 = (f32[512,512]{1,0:T(8,128)S(1)}, bf16[512,512]{1,0:T(8,128)(2,1)S(1)}) custom-call(s32[32]{0:T(128)S(1)} %copy-done.5, bf16[512,512]{1,0:T(8,128)(2,1)S(1)} %copy-done.6, bf16[512,512]{1,0:T(8,128)(2,1)S(1)} %copy-done.1, bf16[512,512]{1,0:T(8,128)(2,1)S(1)} %copy-done.3, f32[512,4]{1,0:T(8,128)S(1)} %copy.7.decay_ref), custom_call_target="tpu_custom_call" | custom-call | flops 536870912 | bytes 2359296 | tf_op jit(solution)/shard_map/within/pallas_call | solution.py:157
  51.1 11.9 %all-to-all-done.1 = bf16[32,16,128]{2,1,0:T(8,128)(2,1)S(1)} async-done(((bf16[32,16,128]{2,1,0:T(8,128)(2,1)}), bf16[32,16,128]{2,1,0:T(8,128)(2,1)S(1)}, u32[]{:S(2)}, u32[]{:S(2)}) %all-to-all-start.1) | async-done | bytes 131104 | tf_op jit(solution)/shard_map/all_to_all | solution.py:176
  63.0 0.0 copy-start.4
  63.0 0.7 copy-done.4
  63.7 1.2 %finish.1 = bf16[512,512]{1,0:T(8,128)(2,1)S(1)} custom-call(f32[512,512]{1,0:T(8,128)S(1)} %get-tuple-element.7.within_ref, bf16[512,512]{1,0:T(8,128)(2,1)S(1)} %get-tuple-element.8.decayed_ref, bf16[512,128]{1,0:T(8,128)(2,1)S(1)} %bitcast.7, f32[1,512]{1,0:T(1,128)S(1)} %bitcast.8), custom_call_target="tpu_custom_call" | custom-call | tf_op jit(solution)/shard_map/finish/pallas_call | solution.py:178
  64.9 16.9 %all_to_all.30 = bf16[8,64,512]{2,1,0:T(8,128)(2,1)S(1)} all-to-all(bf16[8,64,512]{2,1,0:T(8,128)(2,1)S(1)} %bitcast.6), channel_id=1, replica_groups=mesh['seq'=64,'section'=8] {'section'}, dimensions={0} | all-to-all | bytes 1048576 | tf_op jit(solution)/shard_map/all_to_all | solution.py:192
  81.8 0.8 %copy.10 = bf16[8,8,8,512]{3,2,0,1:T(8,128)(2,1)} copy(bf16[8,8,8,512]{3,2,1,0:T(8,128)(2,1)S(1)} %bitcast.9) | data formatting | bytes 1048576 | tf_op jit(solution)/shard_map/all_to_all | solution.py:192
Async XLA Ops:
  0.0 0.9 %copy-start.5 = (s32[32]{0:T(128)S(1)}, s32[32]{0:T(128)}, u32[]{:S(2)}) copy-start(s32[32]{0:T(128)} %lengths_ref.3) | copy-start | bytes 388
  0.9 1.0 %copy-start = (bf16[512,512]{1,0:T(8,128)(2,1)S(1)}, bf16[512,512]{1,0:T(8,128)(2,1)}, u32[]{:S(2)}) copy-start(bf16[512,512]{1,0:T(8,128)(2,1)} %key_ref.3) | copy-start | bytes 1572868
  1.9 1.0 %copy-start.2 = (bf16[512,512]{1,0:T(8,128)(2,1)S(1)}, bf16[512,512]{1,0:T(8,128)(2,1)}, u32[]{:S(2)}) copy-start(bf16[512,512]{1,0:T(8,128)(2,1)} %value_ref.3) | copy-start | bytes 1572868
  3.0 44.4 %copy-start.3 = (bf16[512,512]{1,0:T(8,128)(2,1)S(1)}, bf16[512,512]{1,0:T(8,128)(2,1)}, u32[]{:S(2)}) copy-start(bf16[512,512]{1,0:T(8,128)(2,1)} %value_ref.3) | copy-start | bytes 1572868
  3.0 44.4 %copy-start.6 = (bf16[512,512]{1,0:T(8,128)(2,1)S(1)}, bf16[512,512]{1,0:T(8,128)(2,1)}, u32[]{:S(2)}) copy-start(bf16[512,512]{1,0:T(8,128)(2,1)} %query_ref.1) | copy-start | bytes 1572868
  4.8 42.5 %copy-start.1 = (bf16[512,512]{1,0:T(8,128)(2,1)S(1)}, bf16[512,512]{1,0:T(8,128)(2,1)}, u32[]{:S(2)}) copy-start(bf16[512,512]{1,0:T(8,128)(2,1)} %key_ref.3) | copy-start | bytes 1572868
  42.3 20.7 %all-to-all-start.1 = ((bf16[32,16,128]{2,1,0:T(8,128)(2,1)}), bf16[32,16,128]{2,1,0:T(8,128)(2,1)S(1)}, u32[]{:S(2)}, u32[]{:S(2)}) async-start(bf16[32,16,128]{2,1,0:T(8,128)(2,1)} %scan.1), calls=%async_computation.1 | async-start | bytes 262144 | tf_op jit(solution)/shard_map/all_to_all | solution.py:176
  63.0 0.7 copy-start.4

commit v2 on v1

--- a/solution.py
+++ b/solution.py
@@ -36,38 +36,52 @@
     return start_last, end_prev
 
 
-def state_kernel(lengths_ref, key_ref, value_ref, decay_ref, out_ref):
-    rows, heads = decay_ref.shape
-    dim = key_ref.shape[1] // heads
+def state_kernel(lengths_hbm, key_hbm, value_hbm, decay_hbm, out_ref, lengths_ref, keys_ref, values_ref, decay_ref, sems):
+    heads, rows = decay_ref.shape
+    dim = keys_ref.shape[1] // heads
     holders, slots = out_ref.shape[0], heads * dim // out_ref.shape[0]
-    first_row = lax.axis_index("seq") * rows
-    start_last, _ = document_limits(lengths_ref, first_row, rows)
+    small = [
+        pltpu.make_async_copy(lengths_hbm, lengths_ref, sems.at[2 * heads]),
+        pltpu.make_async_copy(decay_hbm, decay_ref, sems.at[2 * heads + 1]),
+    ]
+    spans = [pl.ds(head * dim, dim) for head in range(heads)]
+    large = []
+    for head, span in enumerate(spans):
+        large.append(pltpu.make_async_copy(key_hbm.at[:, span], keys_ref.at[:, span], sems.at[2 * head]))
+        large.append(pltpu.make_async_copy(value_hbm.at[:, span], values_ref.at[:, span], sems.at[2 * head + 1]))
+    for copy in small + large:
+        copy.start()
     row = lax.broadcasted_iota(jnp.int32, (rows, rows), 0)
     col = lax.broadcasted_iota(jnp.int32, (rows, rows), 1)
     later = (col > row).astype(F32).astype(BF16)
-    decay = decay_ref[...]
-    to_end = sum(dot(later, part, (1, 0)) for part in three_parts(decay))
+    for copy in small:
+        copy.wait()
+    first_row = lax.axis_index("seq") * rows
+    start_last, _ = document_limits(lengths_ref, first_row, rows)
+    parts = three_parts(decay_ref[...])
+    to_end = sum(dot(later, part, (1, 1)) for part in parts)
+    all_log = sum(dot(jnp.ones((8, rows), BF16), part, (1, 1)) for part in parts)
     position = first_row + lax.broadcasted_iota(jnp.int32, (rows, 1), 0)
-    in_last = position >= start_last
-    key_scale = jnp.where(in_last, jnp.exp(to_end), 0.0)
-    end_log = to_end[0:1, :] + decay[0:1, :]
-    end_log = jnp.where(start_last >= first_row, NEVER, end_log)
+    key_scale = jnp.where(position >= start_last, jnp.exp(to_end), 0.0)
+    end_log = jnp.where(start_last >= first_row, NEVER, all_log[0:1, :])
     lines = lax.broadcasted_iota(jnp.int32, (DECAY_ROWS, dim), 0)
     per_head = holders // heads
-    for head in range(heads):
-        span = pl.ds(head * dim, dim)
-        keys = (key_ref[:, span].astype(F32) * key_scale[:, head : head + 1]).astype(BF16)
-        state = dot(keys, value_ref[:, span], (0, 0)).astype(BF16)
+    for head, span in enumerate(spans):
         high, mid, low = (p.astype(F32) for p in three_parts(end_log[:, head : head + 1]))
         sent = jnp.where(lines == 0, high, jnp.where(lines == 1, mid, jnp.where(lines == 2, low, 0.0)))
         sent = sent.astype(BF16)
+        large[2 * head].wait()
+        keys = (keys_ref[:, span].astype(F32) * key_scale[:, head : head + 1]).astype(BF16)
+        large[2 * head + 1].wait()
+        state = dot(keys, values_ref[:, span], (0, 0)).astype(BF16)
         for i in range(per_head):
             out_ref[head * per_head + i, 0:slots, :] = state[i * slots : (i + 1) * slots, :]
             out_ref[head * per_head + i, slots : slots + DECAY_ROWS, :] = sent
 
 
-def within_kernel(lengths_ref, query_ref, key_ref, value_ref, decay_ref, within_ref, decayed_ref):
-    rows, heads = decay_ref.shape
+def within_kernel(lengths_ref, query_ref, key_ref, value_ref, decay_ref, gain_ref, within_ref, decayed_ref, staged_ref):
+    heads, rows = decay_ref.shape
+    staged_ref[...] = gain_ref[...]
     dim = key_ref.shape[1] // heads
     scale = 1.0 / math.sqrt(dim)
     step = 128
@@ -77,8 +91,8 @@
     col = lax.broadcasted_iota(jnp.int32, (rows, rows), 1)
     upto = (col <= row).astype(F32).astype(BF16)
     parts = three_parts(decay_ref[...])
-    cumul_col = sum(dot(upto, part, (1, 0)) for part in parts)
-    cumul_row = sum(dot(part, upto, (0, 1)) for part in parts)
+    cumul_col = sum(dot(upto, part, (1, 1)) for part in parts)
+    cumul_row = sum(dot(part, upto, (1, 1)) for part in parts)
     spot_row = first_row + lax.broadcasted_iota(jnp.int32, (1, rows), 1)
     lane = lax.broadcasted_iota(jnp.int32, (1, dim), 1)
     doc_row = jnp.zeros((1, rows), F32)
@@ -128,8 +142,8 @@
         out_ref[:, span] = (attention * lax.rsqrt(mean_square + 1e-05) * gain_ref[:, span]).astype(BF16)
 
 
-def params():
-    return pltpu.CompilerParams(vmem_limit_bytes=32 << 20)
+def params(mib=32):
+    return pltpu.CompilerParams(vmem_limit_bytes=mib << 20)
 
 
 def shards(query_rows, key_rows, value_rows, log_decay, lengths, norm_gain):
@@ -142,29 +156,42 @@
     chains = [middle, [b for b in range(blocks) if b not in middle]]
     holders = len(middle)
     slots = width // holders
+    decay_rows = log_decay.T
+    hbm = pl.BlockSpec(memory_space=pltpu.HBM)
     smem = pl.BlockSpec(memory_space=pltpu.SMEM)
     vmem = pl.BlockSpec(memory_space=pltpu.VMEM)
 
     states = pl.pallas_call(
         state_kernel,
         out_shape=jax.ShapeDtypeStruct((holders, slots + DECAY_ROWS, dim), BF16),
-        in_specs=[smem, vmem, vmem, vmem],
+        in_specs=[hbm, hbm, hbm, hbm],
         out_specs=vmem,
-        compiler_params=params(),
+        scratch_shapes=[
+            pltpu.SMEM(lengths.shape, lengths.dtype),
+            pltpu.VMEM((rows, width), BF16),
+            pltpu.VMEM((rows, width), BF16),
+            pltpu.VMEM((heads, rows), F32),
+            pltpu.SemaphoreType.DMA((2 * heads + 2,)),
+        ],
+        compiler_params=params(60),
         name="states",
-    )(lengths, key_rows, value_rows, log_decay)
+    )(lengths, key_rows, value_rows, decay_rows)
     taken = lax.all_to_all(states, "seq", split_axis=0, concat_axis=0, tiled=True, axis_index_groups=chains)
-    within, decayed = pl.pallas_call(
+    within, decayed, gain = pl.pallas_call(
         within_kernel,
-        out_shape=(jax.ShapeDtypeStruct((rows, width), F32), jax.ShapeDtypeStruct((rows, width), BF16)),
-        in_specs=[smem, vmem, vmem, vmem, vmem],
-        out_specs=(vmem, vmem),
+        out_shape=(
+            jax.ShapeDtypeStruct((rows, width), F32),
+            jax.ShapeDtypeStruct((rows, width), BF16),
+            jax.ShapeDtypeStruct((1, width), F32),
+        ),
+        in_specs=[smem, vmem, vmem, vmem, vmem, vmem],
+        out_specs=(vmem, vmem, vmem),
         compiler_params=params(),
         cost_estimate=pl.CostEstimate(
             flops=4 * rows * rows * width, bytes_accessed=9 * rows * width, transcendentals=rows * rows * heads
         ),
         name="within",
-    )(lengths, query_rows, key_rows, value_rows, log_decay)
+    )(lengths, query_rows, key_rows, value_rows, decay_rows, norm_gain.reshape(1, width))
     given = pl.pallas_call(
         scan_kernel,
         out_shape=jax.ShapeDtypeStruct((holders, slots, dim), BF16),
@@ -174,21 +201,14 @@
         name="scan",
     )(taken)
     incoming = lax.all_to_all(given, "seq", split_axis=0, concat_axis=0, tiled=True, axis_index_groups=chains)
-    step = rows // 4
     normed = pl.pallas_call(
         finish_kernel,
         out_shape=jax.ShapeDtypeStruct((rows, width), BF16),
-        grid=(rows // step,),
-        in_specs=[
-            pl.BlockSpec((step, width), lambda i: (i, 0)),
-            pl.BlockSpec((step, width), lambda i: (i, 0)),
-            pl.BlockSpec((width, dim), lambda i: (0, 0)),
-            pl.BlockSpec((1, width), lambda i: (0, 0)),
-        ],
-        out_specs=pl.BlockSpec((step, width), lambda i: (i, 0)),
+        in_specs=[vmem] * 4,
+        out_specs=vmem,
         compiler_params=params(),
         name="finish",
-    )(within, decayed, incoming.reshape(width, dim), norm_gain.reshape(1, width))
+    )(within, decayed, incoming.reshape(width, dim), gain)
     return lax.all_to_all(normed, "section", split_axis=0, concat_axis=1, tiled=True)
 
 

time: 83.1 us -> 80.9 us (0.974)
  local copies, waits for them, and re-layouts: 4.46 us -> 1.46 us
  Pallas kernels: 7.52 us -> 8.67 us
    unnamed x15 -> x12, local copies, waits for them, and re-layouts: 3.62 us -> 0.62 us
    pallas_call x1, Pallas kernels: 1.88 us -> 3.77 us  [shards(): pl.pallas_call(state_kernel, out_shape=jax.ShapeDtypeStruct((holders, slo...]
  transfers between devices with their start and end apart: 1 -> 1, of which waited for: 1 -> 1; matrix products, arithmetic and copies ran while one was open for 0% -> 0% of each run, Pallas kernels for 4% -> 5%
where the time goes in v2:
time: 80.9 us; the launch traced here: 80.6 us
  blocking collectives  53.9 us (67%)
  waiting for transfers between devices  11.3 us (14%)
  Pallas kernels  8.67 us (11%)
  starting transfers between devices  5.14 us (6%)
  local copies, waits for them, and re-layouts  1.46 us (2%)
    all_to_all x1, blocking collectives, shards(): lax.all_to_all(states, 'seq', split_axis=0, concat_axis=0, tiled=True, ax...  37 us
    all_to_all x1, blocking collectives, shards(): lax.all_to_all(normed, 'section', split_axis=0, concat_axis=1, tiled=True)  16.9 us
    all_to_all x1, waiting for transfers between devices, shards(): lax.all_to_all(given, 'seq', split_axis=0, concat_axis=0, tiled=True, axi...  11.3 us
    all_to_all x1, starting transfers between devices, shards(): lax.all_to_all(given, 'seq', split_axis=0, concat_axis=0, tiled=True, axi...  5.14 us
    pallas_call x1, Pallas kernels, shards(): pl.pallas_call(state_kernel, out_shape=jax.ShapeDtypeStruct((holders, slo...  3.77 us
    pallas_call x1, Pallas kernels, shards(): pl.pallas_call(within_kernel, out_shape=(jax.ShapeDtypeStruct((rows, widt...  3.66 us
  transfers between devices with their start and end apart: 1, of which 1 were waited for; matrix products, arithmetic and copies ran while one was open for 0% of the time, Pallas kernels for 5%

profile of v2, /device:TPU:1, one launch (start us, length us, event | category | flops | bytes accessed | tf_op | source)
XLA Modules:
  0.0 80.6 jit_solution(215912206885409180)
XLA Ops:
  0.0 0.0 copy-start.1
  0.0 0.0 copy-start.4
  0.0 3.8 %states.1 = bf16[32,24,128]{2,1,0:T(8,128)(2,1)} custom-call(s32[32]{0:T(128)} %lengths_hbm.1, bf16[512,512]{1,0:T(8,128)(2,1)} %key_hbm.1, bf16[512,512]{1,0:T(8,128)(2,1)} %value_hbm.1, f32[4,512]{1,0:T(4,128)} %bitcast.9), custom_call_target="tpu_custom_call" | custom-call | tf_op jit(solution)/shard_map/states/pallas_call | solution.py:164
  3.8 0.0 copy-start
  3.8 37.0 %all_to_all.29.taken_ref = bf16[32,24,128]{2,1,0:T(8,128)(2,1)S(1)} all-to-all(bf16[32,24,128]{2,1,0:T(8,128)(2,1)} %states.1), channel_id=1, replica_groups={{128,136,144,152,160,168,176,184,192,200,208,216,224,232,240,248,256,26..., dimensions={0} | all-to-all | bytes 393216 | tf_op jit(solution)/shard_map/all_to_all | solution.py:179
  40.8 0.7 scan.1
  41.5 0.0 copy-start.2
  41.5 0.0 copy-start.5
  41.5 5.1 %all-to-all-start.1 = ((bf16[32,16,128]{2,1,0:T(8,128)(2,1)}), bf16[32,16,128]{2,1,0:T(8,128)(2,1)S(1)}, u32[]{:S(2)}, u32[]{:S(2)}) async-start(bf16[32,16,128]{2,1,0:T(8,128)(2,1)} %scan.1), calls=%async_computation.1 | async-start | bytes 262144 | tf_op jit(solution)/shard_map/all_to_all | solution.py:203
  46.7 0.0 copy-start.3
  46.7 0.0 copy-done.1
  46.7 0.0 copy-done.4
  46.7 0.0 copy-done
  46.7 0.0 copy-done.2
  46.7 0.0 copy-done.5
  46.7 0.6 copy-done.3
  47.3 3.7 %within.1 = (f32[512,512]{1,0:T(8,128)S(1)}, bf16[512,512]{1,0:T(8,128)(2,1)S(1)}, f32[1,512]{1,0:T(1,128)S(1)}) custom-call(s32[32]{0:T(128)S(1)} %copy-done.3, bf16[512,512]{1,0:T(8,128)(2,1)S(1)} %copy-done.4, bf16[512,512]{1,0:T(8,128)(2,1)S(1)} %copy-done, bf16[512,512]{1,0:T(8,128)(2,1)S(1)} %copy-done.1, f32[4,512]{1,0:T(4,128)S(1)} %bitcast.10, ...), custom_call_target="tpu_custom_call" | custom-call | flops 536870912 | bytes 2359296 | tf_op jit(solution)/shard_map/within/pallas_call | solution.py:180
  51.0 11.3 %all-to-all-done.1 = bf16[32,16,128]{2,1,0:T(8,128)(2,1)S(1)} async-done(((bf16[32,16,128]{2,1,0:T(8,128)(2,1)}), bf16[32,16,128]{2,1,0:T(8,128)(2,1)S(1)}, u32[]{:S(2)}, u32[]{:S(2)}) %all-to-all-start.1) | async-done | bytes 131104 | tf_op jit(solution)/shard_map/all_to_all | solution.py:203
  62.3 0.5 finish.1
  62.8 16.9 %all_to_all.30 = bf16[8,64,512]{2,1,0:T(8,128)(2,1)S(1)} all-to-all(bf16[8,64,512]{2,1,0:T(8,128)(2,1)S(1)} %bitcast.7), channel_id=1, replica_groups=mesh['seq'=64,'section'=8] {'section'}, dimensions={0} | all-to-all | bytes 1048576 | tf_op jit(solution)/shard_map/all_to_all | solution.py:212
  79.7 0.8 %copy.8 = bf16[8,8,8,512]{3,2,0,1:T(8,128)(2,1)} copy(bf16[8,8,8,512]{3,2,1,0:T(8,128)(2,1)S(1)} %bitcast.12) | data formatting | bytes 1048576 | tf_op jit(solution)/shard_map/all_to_all | solution.py:212
Async XLA Ops:
  0.0 46.7 %copy-start.1 = (bf16[512,512]{1,0:T(8,128)(2,1)S(1)}, bf16[512,512]{1,0:T(8,128)(2,1)}, u32[]{:S(2)}) copy-start(bf16[512,512]{1,0:T(8,128)(2,1)} %value_hbm.1) | copy-start | bytes 1572868
  0.0 46.7 %copy-start.4 = (bf16[512,512]{1,0:T(8,128)(2,1)S(1)}, bf16[512,512]{1,0:T(8,128)(2,1)}, u32[]{:S(2)}) copy-start(bf16[512,512]{1,0:T(8,128)(2,1)} %query_ref.1) | copy-start | bytes 1572868
  3.8 42.9 %copy-start = (bf16[512,512]{1,0:T(8,128)(2,1)S(1)}, bf16[512,512]{1,0:T(8,128)(2,1)}, u32[]{:S(2)}) copy-start(bf16[512,512]{1,0:T(8,128)(2,1)} %key_hbm.1) | copy-start | bytes 1572868
  41.5 5.2 %copy-start.2 = (f32[512,4]{0,1:T(4,128)S(1)}, f32[512,4]{0,1:T(4,128)}, u32[]{:S(2)}) copy-start(f32[512,4]{0,1:T(4,128)} %param.9) | copy-start | bytes 24580
  41.5 5.2 %copy-start.5 = (f32[512]{0:T(512)S(1)}, f32[512]{0:T(512)}, u32[]{:S(2)}) copy-start(f32[512]{0:T(512)} %param.11) | copy-start | bytes 6148
  41.5 20.8 %all-to-all-start.1 = ((bf16[32,16,128]{2,1,0:T(8,128)(2,1)}), bf16[32,16,128]{2,1,0:T(8,128)(2,1)S(1)}, u32[]{:S(2)}, u32[]{:S(2)}) async-start(bf16[32,16,128]{2,1,0:T(8,128)(2,1)} %scan.1), calls=%async_computation.1 | async-start | bytes 262144 | tf_op jit(solution)/shard_map/all_to_all | solution.py:203
  46.7 0.7 copy-start.3

commit v3 on v2

--- a/solution.py
+++ b/solution.py
@@ -9,7 +9,7 @@
 
 F32, BF16 = jnp.float32, jnp.bfloat16
 NEVER = -1e30
-DECAY_ROWS = 8
+PAIR = 2
 
 
 def dot(a, b, contract):
@@ -64,19 +64,21 @@
     position = first_row + lax.broadcasted_iota(jnp.int32, (rows, 1), 0)
     key_scale = jnp.where(position >= start_last, jnp.exp(to_end), 0.0)
     end_log = jnp.where(start_last >= first_row, NEVER, all_log[0:1, :])
-    lines = lax.broadcasted_iota(jnp.int32, (DECAY_ROWS, dim), 0)
+    lane = lax.broadcasted_iota(jnp.int32, (PAIR, dim), 1)
     per_head = holders // heads
     for head, span in enumerate(spans):
         high, mid, low = (p.astype(F32) for p in three_parts(end_log[:, head : head + 1]))
-        sent = jnp.where(lines == 0, high, jnp.where(lines == 1, mid, jnp.where(lines == 2, low, 0.0)))
+        sent = jnp.where(lane == 0, high, jnp.where(lane == 1, mid, jnp.where(lane == 2, low, 0.0)))
         sent = sent.astype(BF16)
         large[2 * head].wait()
         keys = (keys_ref[:, span].astype(F32) * key_scale[:, head : head + 1]).astype(BF16)
         large[2 * head + 1].wait()
         state = dot(keys, values_ref[:, span], (0, 0)).astype(BF16)
         for i in range(per_head):
-            out_ref[head * per_head + i, 0:slots, :] = state[i * slots : (i + 1) * slots, :]
-            out_ref[head * per_head + i, slots : slots + DECAY_ROWS, :] = sent
+            for pair in range(slots // PAIR):
+                at = i * slots + pair * PAIR
+                out_ref[head * per_head + i, pair] = state[at : at + PAIR, :]
+            out_ref[head * per_head + i, slots // PAIR] = sent
 
 
 def within_kernel(lengths_ref, query_ref, key_ref, value_ref, decay_ref, gain_ref, within_ref, decayed_ref, staged_ref):
@@ -122,14 +124,25 @@
             within_ref[pl.ds(at, step), span] = dot(weights, value_ref[pl.ds(0, upper), span], (1, 0))
 
 
-def scan_kernel(taken_ref, out_ref):
-    blocks, slots, dim = out_ref.shape
-    carry = jnp.zeros((slots, dim), F32)
+def kept_of(taken_ref, block):
+    parts = taken_ref[block, taken_ref.shape[1] - 1].astype(F32)[0:1, 0:3]
+    return jnp.exp(jnp.sum(parts, axis=1, keepdims=True))
+
+
+def total_kernel(taken_ref, total_ref):
+    blocks, pairs = taken_ref.shape[0], taken_ref.shape[1] - 1
+    carry = jnp.zeros(total_ref.shape, F32)
+    for block in range(blocks):
+        carry = taken_ref[block, 0:pairs].astype(F32) + kept_of(taken_ref, block) * carry
+    total_ref[...] = carry
+
+
+def scan_kernel(taken_ref, entering_ref, out_ref):
+    blocks, pairs = taken_ref.shape[0], taken_ref.shape[1] - 1
+    carry = entering_ref[...]
     for block in range(blocks):
         out_ref[block] = carry.astype(BF16)
-        tail = taken_ref[block, slots : slots + DECAY_ROWS, :].astype(F32)
-        kept = jnp.exp(tail[0:1] + tail[1:2] + tail[2:3])
-        carry = taken_ref[block, 0:slots, :].astype(F32) + kept * carry
+        carry = taken_ref[block, 0:pairs].astype(F32) + kept_of(taken_ref, block) * carry
 
 
 def finish_kernel(within_ref, decayed_ref, incoming_ref, gain_ref, out_ref):
@@ -150,12 +163,11 @@
     rows, width = query_rows.shape
     heads = log_decay.shape[1]
     dim = width // heads
-    blocks = lax.axis_size("seq")
-    quarter = blocks // 4
-    middle = list(range(quarter, 3 * quarter))
-    chains = [middle, [b for b in range(blocks) if b not in middle]]
-    holders = len(middle)
+    holders = lax.axis_size("seq") // 4
+    chains = [list(range(at, at + holders)) for at in range(0, 4 * holders, holders)]
+    onward = [(holders + i, 2 * holders + i) for i in range(holders)]
     slots = width // holders
+    pairs = slots // PAIR
     decay_rows = log_decay.T
     hbm = pl.BlockSpec(memory_space=pltpu.HBM)
     smem = pl.BlockSpec(memory_space=pltpu.SMEM)
@@ -163,7 +175,7 @@
 
     states = pl.pallas_call(
         state_kernel,
-        out_shape=jax.ShapeDtypeStruct((holders, slots + DECAY_ROWS, dim), BF16),
+        out_shape=jax.ShapeDtypeStruct((holders, pairs + 1, PAIR, dim), BF16),
         in_specs=[hbm, hbm, hbm, hbm],
         out_specs=vmem,
         scratch_shapes=[
@@ -192,14 +204,23 @@
         ),
         name="within",
     )(lengths, query_rows, key_rows, value_rows, decay_rows, norm_gain.reshape(1, width))
+    total = pl.pallas_call(
+        total_kernel,
+        out_shape=jax.ShapeDtypeStruct((pairs, PAIR, dim), F32),
+        in_specs=[vmem],
+        out_specs=vmem,
+        compiler_params=params(),
+        name="total",
+    )(taken)
+    entering = lax.ppermute(total, "seq", onward)
     given = pl.pallas_call(
         scan_kernel,
-        out_shape=jax.ShapeDtypeStruct((holders, slots, dim), BF16),
-        in_specs=[vmem],
+        out_shape=jax.ShapeDtypeStruct((holders, pairs, PAIR, dim), BF16),
+        in_specs=[vmem, vmem],
         out_specs=vmem,
         compiler_params=params(),
         name="scan",
-    )(taken)
+    )(taken, entering)
     incoming = lax.all_to_all(given, "seq", split_axis=0, concat_axis=0, tiled=True, axis_index_groups=chains)
     normed = pl.pallas_call(
         finish_kernel,

time: 80.9 us -> 74.6 us (0.922)
  the two profiles are of different devices: /device:TPU:1 before, /device:TPU:16 now
where the time goes in v3:
time: 74.6 us; the launch traced here: 74.2 us
  blocking collectives  44.8 us (60%)
  waiting for transfers between devices  13.5 us (18%)
  Pallas kernels  9.02 us (12%)
  starting transfers between devices  5.38 us (7%)
  local copies, waits for them, and re-layouts  1.46 us (2%)
    all_to_all x1, blocking collectives, shards(): lax.all_to_all(states, 'seq', split_axis=0, concat_axis=0, tiled=True, ax...  30.3 us
    all_to_all x1, blocking collectives, shards(): lax.all_to_all(normed, 'section', split_axis=0, concat_axis=1, tiled=True)  14.5 us
    all_to_all x1, waiting for transfers between devices, shards(): lax.all_to_all(given, 'seq', split_axis=0, concat_axis=0, tiled=True, axi...  9.13 us
    ppermute x1, waiting for transfers between devices, shards(): entering = lax.ppermute(total, 'seq', onward)  4.33 us
    all_to_all x1, starting transfers between devices, shards(): lax.all_to_all(given, 'seq', split_axis=0, concat_axis=0, tiled=True, axi...  4.09 us
    pallas_call x1, Pallas kernels, shards(): pl.pallas_call(state_kernel, out_shape=jax.ShapeDtypeStruct((holders, pai...  3.78 us
    pallas_call x1, Pallas kernels, shards(): pl.pallas_call(within_kernel, out_shape=(jax.ShapeDtypeStruct((rows, widt...  3.66 us
  transfers between devices with their start and end apart: 2, of which 2 were waited for; matrix products, arithmetic and copies ran while one was open for 0% of the time, Pallas kernels for 5%

profile of v3, /device:TPU:16, one launch (start us, length us, event | category | flops | bytes accessed | tf_op | source)
XLA Modules:
  0.0 74.2 jit_solution(10662051888154730418)
XLA Ops:
  0.0 0.0 copy-start.1
  0.0 0.0 copy-start.4
  0.0 3.8 %states.1 = bf16[16,17,2,128]{3,2,1,0:T(2,128)(2,1)} custom-call(s32[32]{0:T(128)} %lengths_hbm.1, bf16[512,512]{1,0:T(8,128)(2,1)} %key_hbm.1, bf16[512,512]{1,0:T(8,128)(2,1)} %value_hbm.1, f32[4,512]{1,0:T(4,128)} %bitcast.9), custom_call_target="tpu_custom_call" | custom-call | tf_op jit(solution)/shard_map/states/pallas_call | solution.py:176
  3.8 0.0 copy-start
  3.8 30.3 %all_to_all.29.taken_ref = bf16[16,17,2,128]{3,2,1,0:T(2,128)(2,1)S(1)} all-to-all(bf16[16,17,2,128]{3,2,1,0:T(2,128)(2,1)} %states.1), channel_id=1, replica_groups={{0,8,16,24,32,40,48,56,64,72,80,88,96,104,112,120},{128,136,144,152,160..., dimensions={0} | all-to-all | bytes 278528 | tf_op jit(solution)/shard_map/all_to_all | solution.py:191
  34.1 0.2 total.1
  34.3 1.3 %collective-permute-start = (f32[16,2,128]{2,1,0:T(2,128)S(1)}, f32[16,2,128]{2,1,0:T(2,128)S(1)}, u32[]{:S(2)}, u32[]{:S(2)}) collective-permute-start(f32[16,2,128]{2,1,0:T(2,128)S(1)} %total.1), channel_id=1, source_target_pairs={{128,256},{136,264},{144,272},{152,280},{160,288},{168,296},{176,3... | collective-permute-start | bytes 49160 | tf_op jit(solution)/shard_map/ppermute | solution.py:215
  35.6 4.3 %collective-permute-done.entering_ref = f32[16,2,128]{2,1,0:T(2,128)S(1)} collective-permute-done((f32[16,2,128]{2,1,0:T(2,128)S(1)}, f32[16,2,128]{2,1,0:T(2,128)S(1)}, u32[]{:S(2)}, u32[]{:S(2)}) %collective-permute-start) | collective-permute-done | bytes 16416 | tf_op jit(solution)/shard_map/ppermute | solution.py:215
  39.9 0.9 %scan.1 = bf16[16,16,2,128]{3,2,1,0:T(2,128)(2,1)} custom-call(bf16[16,17,2,128]{3,2,1,0:T(2,128)(2,1)S(1)} %all_to_all.29.taken_ref, f32[16,2,128]{2,1,0:T(2,128)S(1)} %collective-permute-done.entering_ref), custom_call_target="tpu_custom_call" | custom-call | tf_op jit(solution)/shard_map/scan/pallas_call | solution.py:216
  40.8 0.0 copy-start.2
  40.8 0.0 copy-start.5
  40.8 4.1 %all-to-all-start.1 = ((bf16[16,16,2,128]{3,2,1,0:T(2,128)(2,1)}), bf16[16,16,2,128]{3,2,1,0:T(2,128)(2,1)S(1)}, u32[]{:S(2)}, u32[]{:S(2)}) async-start(bf16[16,16,2,128]{3,2,1,0:T(2,128)(2,1)} %scan.1), calls=%async_computation.1 | async-start | bytes 262144 | tf_op jit(solution)/shard_map/all_to_all | solution.py:224
  44.9 0.0 copy-start.3
  44.9 0.0 copy-done.1
  44.9 0.0 copy-done.4
  44.9 0.0 copy-done
  44.9 0.0 copy-done.2
  44.9 0.0 copy-done.5
  44.9 0.6 copy-done.3
  45.5 3.7 %within.1 = (f32[512,512]{1,0:T(8,128)S(1)}, bf16[512,512]{1,0:T(8,128)(2,1)S(1)}, f32[1,512]{1,0:T(1,128)S(1)}) custom-call(s32[32]{0:T(128)S(1)} %copy-done.3, bf16[512,512]{1,0:T(8,128)(2,1)S(1)} %copy-done.4, bf16[512,512]{1,0:T(8,128)(2,1)S(1)} %copy-done, bf16[512,512]{1,0:T(8,128)(2,1)S(1)} %copy-done.1, f32[4,512]{1,0:T(4,128)S(1)} %bitcast.10, ...), custom_call_target="tpu_custom_call" | custom-call | flops 536870912 | bytes 2359296 | tf_op jit(solution)/shard_map/within/pallas_call | solution.py:192
  49.2 9.1 %all-to-all-done.1 = bf16[16,16,2,128]{3,2,1,0:T(2,128)(2,1)S(1)} async-done(((bf16[16,16,2,128]{3,2,1,0:T(2,128)(2,1)}), bf16[16,16,2,128]{3,2,1,0:T(2,128)(2,1)S(1)}, u32[]{:S(2)}, u32[]{:S(2)}) %all-to-all-start.1) | async-done | bytes 131104 | tf_op jit(solution)/shard_map/all_to_all | solution.py:224
  58.3 0.5 finish.1
  58.9 14.5 %all_to_all.30 = bf16[8,64,512]{2,1,0:T(8,128)(2,1)S(1)} all-to-all(bf16[8,64,512]{2,1,0:T(8,128)(2,1)S(1)} %bitcast.7), channel_id=1, replica_groups=mesh['seq'=64,'section'=8] {'section'}, dimensions={0} | all-to-all | bytes 1048576 | tf_op jit(solution)/shard_map/all_to_all | solution.py:233
  73.4 0.8 %copy.8 = bf16[8,8,8,512]{3,2,0,1:T(8,128)(2,1)} copy(bf16[8,8,8,512]{3,2,1,0:T(8,128)(2,1)S(1)} %bitcast.12) | data formatting | bytes 1048576 | tf_op jit(solution)/shard_map/all_to_all | solution.py:233
Async XLA Ops:
  0.0 44.9 %copy-start.1 = (bf16[512,512]{1,0:T(8,128)(2,1)S(1)}, bf16[512,512]{1,0:T(8,128)(2,1)}, u32[]{:S(2)}) copy-start(bf16[512,512]{1,0:T(8,128)(2,1)} %value_hbm.1) | copy-start | bytes 1572868
  0.0 44.9 %copy-start.4 = (bf16[512,512]{1,0:T(8,128)(2,1)S(1)}, bf16[512,512]{1,0:T(8,128)(2,1)}, u32[]{:S(2)}) copy-start(bf16[512,512]{1,0:T(8,128)(2,1)} %query_ref.1) | copy-start | bytes 1572868
  3.8 41.1 %copy-start = (bf16[512,512]{1,0:T(8,128)(2,1)S(1)}, bf16[512,512]{1,0:T(8,128)(2,1)}, u32[]{:S(2)}) copy-start(bf16[512,512]{1,0:T(8,128)(2,1)} %key_hbm.1) | copy-start | bytes 1572868
  34.3 5.6 %collective-permute-start = (f32[16,2,128]{2,1,0:T(2,128)S(1)}, f32[16,2,128]{2,1,0:T(2,128)S(1)}, u32[]{:S(2)}, u32[]{:S(2)}) collective-permute-start(f32[16,2,128]{2,1,0:T(2,128)S(1)} %total.1), channel_id=1, source_target_pairs={{128,256},{136,264},{144,272},{152,280},{160,288},{168,296},{176,3... | collective-permute-start | bytes 49160 | tf_op jit(solution)/shard_map/ppermute | solution.py:215
  40.8 4.1 %copy-start.2 = (f32[512,4]{0,1:T(4,128)S(1)}, f32[512,4]{0,1:T(4,128)}, u32[]{:S(2)}) copy-start(f32[512,4]{0,1:T(4,128)} %param.9) | copy-start | bytes 24580
  40.8 4.2 %copy-start.5 = (f32[512]{0:T(512)S(1)}, f32[512]{0:T(512)}, u32[]{:S(2)}) copy-start(f32[512]{0:T(512)} %param.11) | copy-start | bytes 6148
  40.8 17.6 %all-to-all-start.1 = ((bf16[16,16,2,128]{3,2,1,0:T(2,128)(2,1)}), bf16[16,16,2,128]{3,2,1,0:T(2,128)(2,1)S(1)}, u32[]{:S(2)}, u32[]{:S(2)}) async-start(bf16[16,16,2,128]{3,2,1,0:T(2,128)(2,1)} %scan.1), calls=%async_computation.1 | async-start | bytes 262144 | tf_op jit(solution)/shard_map/all_to_all | solution.py:224
  44.9 0.7 copy-start.3

commit v4 on v3

--- a/solution.py
+++ b/solution.py
@@ -10,6 +10,7 @@
 F32, BF16 = jnp.float32, jnp.bfloat16
 NEVER = -1e30
 PAIR = 2
+CHUNK = 128
 
 
 def dot(a, b, contract):
@@ -40,49 +41,68 @@
     heads, rows = decay_ref.shape
     dim = keys_ref.shape[1] // heads
     holders, slots = out_ref.shape[0], heads * dim // out_ref.shape[0]
+    chunks = rows // CHUNK
     small = [
-        pltpu.make_async_copy(lengths_hbm, lengths_ref, sems.at[2 * heads]),
-        pltpu.make_async_copy(decay_hbm, decay_ref, sems.at[2 * heads + 1]),
+        pltpu.make_async_copy(decay_hbm, decay_ref, sems.at[0]),
+        pltpu.make_async_copy(lengths_hbm, lengths_ref, sems.at[1]),
     ]
-    spans = [pl.ds(head * dim, dim) for head in range(heads)]
-    large = []
-    for head, span in enumerate(spans):
-        large.append(pltpu.make_async_copy(key_hbm.at[:, span], keys_ref.at[:, span], sems.at[2 * head]))
-        large.append(pltpu.make_async_copy(value_hbm.at[:, span], values_ref.at[:, span], sems.at[2 * head + 1]))
-    for copy in small + large:
+    spans = [pl.ds(c * CHUNK, CHUNK) for c in range(chunks)]
+    keys_in = [pltpu.make_async_copy(key_hbm.at[at], keys_ref.at[at], sems.at[2 + 2 * c]) for c, at in enumerate(spans)]
+    values_in = [pltpu.make_async_copy(value_hbm.at[at], values_ref.at[at], sems.at[3 + 2 * c]) for c, at in enumerate(spans)]
+    for copy in small:
         copy.start()
-    row = lax.broadcasted_iota(jnp.int32, (rows, rows), 0)
-    col = lax.broadcasted_iota(jnp.int32, (rows, rows), 1)
-    later = (col > row).astype(F32).astype(BF16)
-    for copy in small:
-        copy.wait()
+    for c in range(chunks):
+        keys_in[c].start()
+        values_in[c].start()
+    row = lax.broadcasted_iota(jnp.int32, (CHUNK, CHUNK), 0)
+    col = lax.broadcasted_iota(jnp.int32, (CHUNK, CHUNK), 1)
+    later = (row > col).astype(F32).astype(BF16)
+    small[0].wait()
+    decay = jnp.concatenate([decay_ref[:, c * CHUNK : (c + 1) * CHUNK] for c in range(chunks)], axis=0)
+    suffix = sum(dot(part, later, (1, 0)) for part in three_parts(decay))
+    chunk_log = suffix[:, 0:1] + decay[:, 0:1]
+    small[1].wait()
     first_row = lax.axis_index("seq") * rows
     start_last, _ = document_limits(lengths_ref, first_row, rows)
-    parts = three_parts(decay_ref[...])
-    to_end = sum(dot(later, part, (1, 1)) for part in parts)
-    all_log = sum(dot(jnp.ones((8, rows), BF16), part, (1, 1)) for part in parts)
-    position = first_row + lax.broadcasted_iota(jnp.int32, (rows, 1), 0)
-    key_scale = jnp.where(position >= start_last, jnp.exp(to_end), 0.0)
-    end_log = jnp.where(start_last >= first_row, NEVER, all_log[0:1, :])
+    scales = [None] * chunks
+    end_log = jnp.zeros((heads, 1), F32)
+    for c in reversed(range(chunks)):
+        mine = slice(c * heads, (c + 1) * heads)
+        position = first_row + c * CHUNK + lax.broadcasted_iota(jnp.int32, (1, CHUNK), 1)
+        scales[c] = jnp.where(position >= start_last, jnp.exp(suffix[mine] + end_log), 0.0)
+        end_log = end_log + chunk_log[mine]
+    end_log = jnp.where(start_last >= first_row, NEVER, end_log)
+    high, mid, low = (part.astype(F32) for part in three_parts(end_log))
     lane = lax.broadcasted_iota(jnp.int32, (PAIR, dim), 1)
     per_head = holders // heads
-    for head, span in enumerate(spans):
-        high, mid, low = (p.astype(F32) for p in three_parts(end_log[:, head : head + 1]))
-        sent = jnp.where(lane == 0, high, jnp.where(lane == 1, mid, jnp.where(lane == 2, low, 0.0)))
-        sent = sent.astype(BF16)
-        large[2 * head].wait()
-        keys = (keys_ref[:, span].astype(F32) * key_scale[:, head : head + 1]).astype(BF16)
-        large[2 * head + 1].wait()
-        state = dot(keys, values_ref[:, span], (0, 0)).astype(BF16)
+    scale = jnp.concatenate(scales, axis=1)
+    for copy in keys_in + values_in:
+        copy.wait()
+    for head in range(heads):
+        one = slice(head, head + 1)
+        sent = jnp.where(lane == 0, high[one], jnp.where(lane == 1, mid[one], jnp.where(lane == 2, low[one], 0.0)))
+        span = pl.ds(head * dim, dim)
+        keys = (keys_ref[:, span].T.astype(F32) * scale[one, :]).astype(BF16)
+        state = dot(keys, values_ref[:, span], (1, 0)).astype(BF16)
         for i in range(per_head):
             for pair in range(slots // PAIR):
                 at = i * slots + pair * PAIR
                 out_ref[head * per_head + i, pair] = state[at : at + PAIR, :]
-            out_ref[head * per_head + i, slots // PAIR] = sent
-
-
-def within_kernel(lengths_ref, query_ref, key_ref, value_ref, decay_ref, gain_ref, within_ref, decayed_ref, staged_ref):
+            out_ref[head * per_head + i, slots // PAIR] = sent.astype(BF16)
+
+
+def within_kernel(
+    lengths_ref, query_hbm, key_hbm, value_hbm, decay_ref, gain_ref,
+    within_ref, decayed_ref, staged_ref, query_ref, key_ref, value_ref, sems,
+):
     heads, rows = decay_ref.shape
+    fetched = [
+        pltpu.make_async_copy(query_hbm, query_ref, sems.at[0]),
+        pltpu.make_async_copy(key_hbm, key_ref, sems.at[1]),
+        pltpu.make_async_copy(value_hbm, value_ref, sems.at[2]),
+    ]
+    for copy in fetched:
+        copy.start()
     staged_ref[...] = gain_ref[...]
     dim = key_ref.shape[1] // heads
     scale = 1.0 / math.sqrt(dim)
@@ -106,6 +126,8 @@
         ends = ends + jnp.where(lane >= doc, lengths_ref[doc], 0)
     position = first_row + lax.broadcasted_iota(jnp.int32, (rows, 1), 0)
     doc_col = jnp.sum(jnp.where(ends <= position, 1.0, 0.0), axis=1, keepdims=True)
+    for copy in fetched:
+        copy.wait()
     query_scale = jnp.where(position < end_prev, jnp.exp(cumul_col) * scale, 0.0)
     for head in range(heads):
         span = pl.ds(head * dim, dim)
@@ -137,12 +159,25 @@
     total_ref[...] = carry
 
 
-def scan_kernel(taken_ref, entering_ref, out_ref):
+def prefix_kernel(taken_ref, before_ref, reach_ref):
     blocks, pairs = taken_ref.shape[0], taken_ref.shape[1] - 1
-    carry = entering_ref[...]
+    carry = jnp.zeros(before_ref.shape[1:], F32)
+    reach = jnp.ones((1, 1), F32)
     for block in range(blocks):
-        out_ref[block] = carry.astype(BF16)
-        carry = taken_ref[block, 0:pairs].astype(F32) + kept_of(taken_ref, block) * carry
+        before_ref[block] = carry
+        reach_ref[block] = jnp.broadcast_to(reach, reach_ref.shape[1:])
+        kept = kept_of(taken_ref, block)
+        carry = taken_ref[block, 0:pairs].astype(F32) + kept * carry
+        reach = kept * reach
+
+
+def enter_kernel(before_ref, reach_ref, entering_ref, out_ref):
+    slots = entering_ref.shape[0]
+    entering = entering_ref[...]
+    for block in range(out_ref.shape[0]):
+        at = pl.ds(block * slots, slots)
+        reach = reach_ref[block * PAIR : block * PAIR + 1, :]
+        out_ref[block] = (before_ref[at, :] + reach * entering).astype(BF16)
 
 
 def finish_kernel(within_ref, decayed_ref, incoming_ref, gain_ref, out_ref):
@@ -155,8 +190,12 @@
         out_ref[:, span] = (attention * lax.rsqrt(mean_square + 1e-05) * gain_ref[:, span]).astype(BF16)
 
 
-def params(mib=32):
-    return pltpu.CompilerParams(vmem_limit_bytes=mib << 20)
+def params():
+    return pltpu.CompilerParams(vmem_limit_bytes=32 << 20)
+
+
+def in_hbm(x):
+    return pltpu.with_memory_space_constraint(x, pltpu.HBM)
 
 
 def shards(query_rows, key_rows, value_rows, log_decay, lengths, norm_gain):
@@ -183,11 +222,11 @@
             pltpu.VMEM((rows, width), BF16),
             pltpu.VMEM((rows, width), BF16),
             pltpu.VMEM((heads, rows), F32),
-            pltpu.SemaphoreType.DMA((2 * heads + 2,)),
+            pltpu.SemaphoreType.DMA((2 * (rows // CHUNK) + 2,)),
         ],
-        compiler_params=params(60),
+        compiler_params=params(),
         name="states",
-    )(lengths, key_rows, value_rows, decay_rows)
+    )(*(in_hbm(x) for x in (lengths, key_rows, value_rows, decay_rows)))
     taken = lax.all_to_all(states, "seq", split_axis=0, concat_axis=0, tiled=True, axis_index_groups=chains)
     within, decayed, gain = pl.pallas_call(
         within_kernel,
@@ -196,14 +235,16 @@
             jax.ShapeDtypeStruct((rows, width), BF16),
             jax.ShapeDtypeStruct((1, width), F32),
         ),
-        in_specs=[smem, vmem, vmem, vmem, vmem, vmem],
+        in_specs=[smem, hbm, hbm, hbm, vmem, vmem],
         out_specs=(vmem, vmem, vmem),
+        scratch_shapes=[pltpu.VMEM((rows, width), BF16)] * 3 + [pltpu.SemaphoreType.DMA((3,))],
         compiler_params=params(),
         cost_estimate=pl.CostEstimate(
             flops=4 * rows * rows * width, bytes_accessed=9 * rows * width, transcendentals=rows * rows * heads
         ),
         name="within",
-    )(lengths, query_rows, key_rows, value_rows, decay_rows, norm_gain.reshape(1, width))
+    )(lengths, *(in_hbm(x) for x in (query_rows, key_rows, value_rows)), decay_rows, norm_gain.reshape(1, width))
+    taken, within, decayed, gain = lax.optimization_barrier((taken, within, decayed, gain))
     total = pl.pallas_call(
         total_kernel,
         out_shape=jax.ShapeDtypeStruct((pairs, PAIR, dim), F32),
@@ -213,14 +254,26 @@
         name="total",
     )(taken)
     entering = lax.ppermute(total, "seq", onward)
+    before, reach = pl.pallas_call(
+        prefix_kernel,
+        out_shape=(
+            jax.ShapeDtypeStruct((holders, pairs, PAIR, dim), F32),
+            jax.ShapeDtypeStruct((holders, PAIR, dim), F32),
+        ),
+        in_specs=[vmem],
+        out_specs=(vmem, vmem),
+        compiler_params=params(),
+        cost_estimate=pl.CostEstimate(flops=2 * width * dim, bytes_accessed=6 * width * dim, transcendentals=holders),
+        name="prefix",
+    )(taken)
     given = pl.pallas_call(
-        scan_kernel,
-        out_shape=jax.ShapeDtypeStruct((holders, pairs, PAIR, dim), BF16),
-        in_specs=[vmem, vmem],
+        enter_kernel,
+        out_shape=jax.ShapeDtypeStruct((holders, slots, dim), BF16),
+        in_specs=[vmem] * 3,
         out_specs=vmem,
         compiler_params=params(),
-        name="scan",
-    )(taken, entering)
+        name="enter",
+    )(before.reshape(width, dim), reach.reshape(holders * PAIR, dim), entering.reshape(slots, dim))
     incoming = lax.all_to_all(given, "seq", split_axis=0, concat_axis=0, tiled=True, axis_index_groups=chains)
     normed = pl.pallas_call(
         finish_kernel,

time: 74.6 us -> 71.9 us (0.964)
  blocking collectives: 44.8 us -> 31.7 us
  starting transfers between devices: 5.38 us -> 16.5 us
  Pallas kernels: 9.02 us -> 8.2 us
    all_to_all x1, blocking collectives: 30.3 us -> 17.2 us  [shards(): lax.all_to_all(given, 'seq', split_axis=0, concat_axis=0, tiled=True, axi...]
    all_to_all x1, starting transfers between devices: 4.09 us -> 15.2 us  [shards(): lax.all_to_all(states, 'seq', split_axis=0, concat_axis=0, tiled=True, ax...]
    pallas_call x1, Pallas kernels: 3.78 us -> 2.4 us  [shards(): pl.pallas_call(state_kernel, out_shape=jax.ShapeDtypeStruct((holders, pai...]
    pallas_call x1, Pallas kernels: 3.66 us -> 4.87 us  [shards(): pl.pallas_call(within_kernel, out_shape=(jax.ShapeDtypeStruct((rows, widt...]
  transfers between devices with their start and end apart: 2 -> 2, of which waited for: 2 -> 2; matrix products, arithmetic and copies ran while one was open for 0% -> 0% of each run, Pallas kernels for 5% -> 7%
where the time goes in v4:
time: 71.9 us; the launch traced here: 71.5 us
  blocking collectives  31.7 us (44%)
  starting transfers between devices  16.5 us (23%)
  waiting for transfers between devices  13.5 us (19%)
  Pallas kernels  8.2 us (11%)
  local copies, waits for them, and re-layouts  1.48 us (2%)
    all_to_all x1, blocking collectives, shards(): lax.all_to_all(given, 'seq', split_axis=0, concat_axis=0, tiled=True, axi...  17.2 us
    all_to_all x1, starting transfers between devices, shards(): lax.all_to_all(states, 'seq', split_axis=0, concat_axis=0, tiled=True, ax...  15.2 us
    all_to_all x1, blocking collectives, shards(): lax.all_to_all(normed, 'section', split_axis=0, concat_axis=1, tiled=True)  14.5 us
    all_to_all x1, waiting for transfers between devices, shards(): lax.all_to_all(states, 'seq', split_axis=0, concat_axis=0, tiled=True, ax...  9.39 us
    pallas_call x1, Pallas kernels, shards(): pl.pallas_call(within_kernel, out_shape=(jax.ShapeDtypeStruct((rows, widt...  4.87 us
    ppermute x1, waiting for transfers between devices, shards(): entering = lax.ppermute(total, 'seq', onward)  4.14 us
    pallas_call x1, Pallas kernels, shards(): pl.pallas_call(state_kernel, out_shape=jax.ShapeDtypeStruct((holders, pai...  2.4 us
  transfers between devices with their start and end apart: 2, of which 2 were waited for; matrix products, arithmetic and copies ran while one was open for 0% of the time, Pallas kernels for 7%

profile of v4, /device:TPU:16, one launch (start us, length us, event | category | flops | bytes accessed | tf_op | source)
XLA Modules:
  0.0 71.5 jit_solution(14135756785893904123)
XLA Ops:
  0.0 2.4 %states.1 = bf16[16,17,2,128]{3,2,1,0:T(2,128)(2,1)} custom-call(s32[32]{0:T(128)} %lengths_ref.1, bf16[512,512]{1,0:T(8,128)(2,1)} %key_hbm.3, bf16[512,512]{1,0:T(8,128)(2,1)} %value_hbm.3, f32[4,512]{1,0:T(4,128)} %bitcast.15), custom_call_target="tpu_custom_call" | custom-call | tf_op jit(solution)/shard_map/states/pallas_call | solution.py:215
  2.4 0.0 copy-start
  2.4 0.0 copy-start.2
  2.4 15.2 %all-to-all-start = ((bf16[16,17,2,128]{3,2,1,0:T(2,128)(2,1)}), bf16[16,17,2,128]{3,2,1,0:T(2,128)(2,1)S(1)}, u32[]{:S(2)}, u32[]{:S(2)}) async-start(bf16[16,17,2,128]{3,2,1,0:T(2,128)(2,1)} %states.1), calls=%async_computation | async-start | bytes 278528 | tf_op jit(solution)/shard_map/all_to_all | solution.py:230
  17.7 0.0 copy-start.1
  17.7 0.0 copy-done
  17.7 0.0 copy-done.2
  17.7 0.6 copy-done.1
  18.3 4.9 %within.1 = (f32[512,512]{1,0:T(8,128)S(1)}, bf16[512,512]{1,0:T(8,128)(2,1)S(1)}, f32[1,512]{1,0:T(1,128)S(1)}) custom-call(s32[32]{0:T(128)S(1)} %copy-done.1, bf16[512,512]{1,0:T(8,128)(2,1)} %query_hbm.1, bf16[512,512]{1,0:T(8,128)(2,1)} %key_hbm.3, bf16[512,512]{1,0:T(8,128)(2,1)} %value_hbm.3, f32[4,512]{1,0:T(4,128)S(1)} %bitcast.16, ...), custom_call_target="tpu_custom_call" | custom-call | flops 536870912 | bytes 2359296 | tf_op jit(solution)/shard_map/within/pallas_call | solution.py:231
  23.2 9.4 %all-to-all-done.taken_ref = bf16[16,17,2,128]{3,2,1,0:T(2,128)(2,1)S(1)} async-done(((bf16[16,17,2,128]{3,2,1,0:T(2,128)(2,1)}), bf16[16,17,2,128]{3,2,1,0:T(2,128)(2,1)S(1)}, u32[]{:S(2)}, u32[]{:S(2)}) %all-to-all-start) | async-done | bytes 139296 | tf_op jit(solution)/shard_map/all_to_all | solution.py:230
  32.6 0.2 total.1
  32.8 1.3 %collective-permute-start = (f32[16,2,128]{2,1,0:T(2,128)S(1)}, f32[16,2,128]{2,1,0:T(2,128)S(1)}, u32[]{:S(2)}, u32[]{:S(2)}) collective-permute-start(f32[16,2,128]{2,1,0:T(2,128)S(1)} %total.1), channel_id=1, source_target_pairs={{128,256},{136,264},{144,272},{152,280},{160,288},{168,296},{176,3... | collective-permute-start | bytes 49160 | tf_op jit(solution)/shard_map/ppermute | solution.py:256
  34.1 0.2 prefix.1
  34.3 4.1 %collective-permute-done = f32[16,2,128]{2,1,0:T(2,128)S(1)} collective-permute-done((f32[16,2,128]{2,1,0:T(2,128)S(1)}, f32[16,2,128]{2,1,0:T(2,128)S(1)}, u32[]{:S(2)}, u32[]{:S(2)}) %collective-permute-start) | collective-permute-done | bytes 16416 | tf_op jit(solution)/shard_map/ppermute | solution.py:256
  38.4 17.2 %all_to_all.29 = bf16[16,32,128]{2,1,0:T(8,128)(2,1)S(1)} all-to-all(bf16[16,32,128]{2,1,0:T(8,128)(2,1)S(1)} %enter.1), channel_id=1, replica_groups={{0,8,16,24,32,40,48,56,64,72,80,88,96,104,112,120},{128,136,144,152,160..., dimensions={0} | all-to-all | bytes 262144 | tf_op jit(solution)/shard_map/all_to_all | solution.py:277
  55.7 0.5 finish.1
  56.2 14.5 %all_to_all.30 = bf16[8,64,512]{2,1,0:T(8,128)(2,1)S(1)} all-to-all(bf16[8,64,512]{2,1,0:T(8,128)(2,1)S(1)} %bitcast.10), channel_id=1, replica_groups=mesh['seq'=64,'section'=8] {'section'}, dimensions={0} | all-to-all | bytes 1048576 | tf_op jit(solution)/shard_map/all_to_all | solution.py:286
  70.7 0.8 %copy.8 = bf16[8,8,8,512]{3,2,0,1:T(8,128)(2,1)} copy(bf16[8,8,8,512]{3,2,1,0:T(8,128)(2,1)S(1)} %bitcast.18) | data formatting | bytes 1048576 | tf_op jit(solution)/shard_map/all_to_all | solution.py:286
  (1 shorter events, 0.0 us)
Async XLA Ops:
  2.4 15.3 %copy-start = (f32[512,4]{0,1:T(4,128)S(1)}, f32[512,4]{0,1:T(4,128)}, u32[]{:S(2)}) copy-start(f32[512,4]{0,1:T(4,128)} %param.9) | copy-start | bytes 24580
  2.4 15.3 %copy-start.2 = (f32[512]{0:T(512)S(1)}, f32[512]{0:T(512)}, u32[]{:S(2)}) copy-start(f32[512]{0:T(512)} %param.11) | copy-start | bytes 6148
  2.4 30.1 %all-to-all-start = ((bf16[16,17,2,128]{3,2,1,0:T(2,128)(2,1)}), bf16[16,17,2,128]{3,2,1,0:T(2,128)(2,1)S(1)}, u32[]{:S(2)}, u32[]{:S(2)}) async-start(bf16[16,17,2,128]{3,2,1,0:T(2,128)(2,1)} %states.1), calls=%async_computation | async-start | bytes 278528 | tf_op jit(solution)/shard_map/all_to_all | solution.py:230
  17.7 0.7 copy-start.1
  32.8 5.6 %collective-permute-start = (f32[16,2,128]{2,1,0:T(2,128)S(1)}, f32[16,2,128]{2,1,0:T(2,128)S(1)}, u32[]{:S(2)}, u32[]{:S(2)}) collective-permute-start(f32[16,2,128]{2,1,0:T(2,128)S(1)} %total.1), channel_id=1, source_target_pairs={{128,256},{136,264},{144,272},{152,280},{160,288},{168,296},{176,3... | collective-permute-start | bytes 49160 | tf_op jit(solution)/shard_map/ppermute | solution.py:256

commit v5 on v4

--- a/solution.py
+++ b/solution.py
@@ -1,3 +1,4 @@
+import functools
 import math
 
 import jax
@@ -11,6 +12,16 @@
 NEVER = -1e30
 PAIR = 2
 CHUNK = 128
+FIRST_Z = 8
+FIRST_SECTION = 4
+
+
+def place(position, count):
+    return (position + FIRST_Z) % count
+
+
+def in_chain(count):
+    return sorted(range(count), key=lambda position: place(position, count))
 
 
 def dot(a, b, contract):
@@ -154,7 +165,7 @@
 def total_kernel(taken_ref, total_ref):
     blocks, pairs = taken_ref.shape[0], taken_ref.shape[1] - 1
     carry = jnp.zeros(total_ref.shape, F32)
-    for block in range(blocks):
+    for block in in_chain(blocks):
         carry = taken_ref[block, 0:pairs].astype(F32) + kept_of(taken_ref, block) * carry
     total_ref[...] = carry
 
@@ -163,7 +174,7 @@
     blocks, pairs = taken_ref.shape[0], taken_ref.shape[1] - 1
     carry = jnp.zeros(before_ref.shape[1:], F32)
     reach = jnp.ones((1, 1), F32)
-    for block in range(blocks):
+    for block in in_chain(blocks):
         before_ref[block] = carry
         reach_ref[block] = jnp.broadcast_to(reach, reach_ref.shape[1:])
         kept = kept_of(taken_ref, block)
@@ -180,14 +191,29 @@
         out_ref[block] = (before_ref[at, :] + reach * entering).astype(BF16)
 
 
-def finish_kernel(within_ref, decayed_ref, incoming_ref, gain_ref, out_ref):
+def finish_kernel(sections, within_ref, decayed_ref, incoming_ref, gain_ref, out_ref):
     dim = incoming_ref.shape[1]
+    tokens = out_ref.shape[1]
     for head in range(incoming_ref.shape[0] // dim):
         span = pl.ds(head * dim, dim)
         carried = dot(decayed_ref[:, span], incoming_ref[span, :], (1, 0))
         attention = within_ref[:, span] + carried
         mean_square = jnp.mean(attention * attention, axis=1, keepdims=True)
-        out_ref[:, span] = (attention * lax.rsqrt(mean_square + 1e-05) * gain_ref[:, span]).astype(BF16)
+        normed = (attention * lax.rsqrt(mean_square + 1e-05) * gain_ref[:, span]).astype(BF16)
+        for i, section in enumerate(sections):
+            out_ref[i, :, span] = normed[section * tokens : (section + 1) * tokens, :]
+
+
+def place_kernel(sections, landed_ref, out_hbm, sems):
+    width = landed_ref.shape[2]
+    copies = [
+        pltpu.make_async_copy(landed_ref.at[i], out_hbm.at[:, pl.ds(section * width, width)], sems.at[i])
+        for i, section in enumerate(sections)
+    ]
+    for copy in copies:
+        copy.start()
+    for copy in copies:
+        copy.wait()
 
 
 def params():
@@ -203,7 +229,7 @@
     heads = log_decay.shape[1]
     dim = width // heads
     holders = lax.axis_size("seq") // 4
-    chains = [list(range(at, at + holders)) for at in range(0, 4 * holders, holders)]
+    chains = [[at + place(i, holders) for i in range(holders)] for at in range(0, 4 * holders, holders)]
     onward = [(holders + i, 2 * holders + i) for i in range(holders)]
     slots = width // holders
     pairs = slots // PAIR
@@ -275,15 +301,28 @@
         name="enter",
     )(before.reshape(width, dim), reach.reshape(holders * PAIR, dim), entering.reshape(slots, dim))
     incoming = lax.all_to_all(given, "seq", split_axis=0, concat_axis=0, tiled=True, axis_index_groups=chains)
+    count = lax.axis_size("section")
+    sections = [(i + FIRST_SECTION) % count for i in range(count)]
     normed = pl.pallas_call(
-        finish_kernel,
-        out_shape=jax.ShapeDtypeStruct((rows, width), BF16),
+        functools.partial(finish_kernel, sections),
+        out_shape=jax.ShapeDtypeStruct((count, rows // count, width), BF16),
         in_specs=[vmem] * 4,
         out_specs=vmem,
         compiler_params=params(),
         name="finish",
     )(within, decayed, incoming.reshape(width, dim), gain)
-    return lax.all_to_all(normed, "section", split_axis=0, concat_axis=1, tiled=True)
+    landed = lax.all_to_all(
+        normed, "section", split_axis=0, concat_axis=0, tiled=True, axis_index_groups=[sections]
+    )
+    return pl.pallas_call(
+        functools.partial(place_kernel, sections),
+        out_shape=jax.ShapeDtypeStruct((rows // count, count * width), BF16),
+        in_specs=[vmem],
+        out_specs=hbm,
+        scratch_shapes=[pltpu.SemaphoreType.DMA((count,))],
+        compiler_params=params(),
+        name="place",
+    )(landed)
 
 
 def solution(mesh):

time: 71.9 us -> 65.4 us (0.910)
  the two profiles are of different devices: /device:TPU:16 before, /device:TPU:20 now
where the time goes in v5:
time: 65.4 us; the launch traced here: 65.1 us
  blocking collectives  29.7 us (45%)
  starting transfers between devices  20.2 us (31%)
  Pallas kernels  9.05 us (14%)
  waiting for transfers between devices  5.46 us (8%)
    all_to_all x1, starting transfers between devices, shards(): lax.all_to_all(states, 'seq', split_axis=0, concat_axis=0, tiled=True, ax...  18.9 us
    all_to_all x1, blocking collectives, shards(): lax.all_to_all(given, 'seq', split_axis=0, concat_axis=0, tiled=True, axi...  16.9 us
    all_to_all x1, blocking collectives, shards(): lax.all_to_all(normed, 'section', split_axis=0, concat_axis=0, tiled=True...  12.8 us
    pallas_call x1, Pallas kernels, shards(): pl.pallas_call(within_kernel, out_shape=(jax.ShapeDtypeStruct((rows, widt...  4.87 us
    ppermute x1, waiting for transfers between devices, shards(): entering = lax.ppermute(total, 'seq', onward)  4.14 us
    pallas_call x1, Pallas kernels, shards(): pl.pallas_call(state_kernel, out_shape=jax.ShapeDtypeStruct((holders, pai...  2.41 us
    all_to_all x1, waiting for transfers between devices, shards(): lax.all_to_all(states, 'seq', split_axis=0, concat_axis=0, tiled=True, ax...  1.33 us
  transfers between devices with their start and end apart: 2, of which 2 were waited for; matrix products, arithmetic and copies ran while one was open for 0% of the time, Pallas kernels for 8%

profile of v5, /device:TPU:20, one launch (start us, length us, event | category | flops | bytes accessed | tf_op | source)
XLA Modules:
  0.0 65.1 jit_solution(11033253477452776696)
XLA Ops:
  0.0 2.4 %states.1 = bf16[16,17,2,128]{3,2,1,0:T(2,128)(2,1)} custom-call(s32[32]{0:T(128)} %lengths_ref.1, bf16[512,512]{1,0:T(8,128)(2,1)} %key_hbm.3, bf16[512,512]{1,0:T(8,128)(2,1)} %value_hbm.3, f32[4,512]{1,0:T(4,128)} %bitcast.10), custom_call_target="tpu_custom_call" | custom-call | tf_op jit(solution)/shard_map/states/pallas_call | solution.py:241
  2.4 0.0 copy-start
  2.4 0.0 copy-start.2
  2.4 18.9 %all-to-all-start = ((bf16[16,17,2,128]{3,2,1,0:T(2,128)(2,1)}), bf16[16,17,2,128]{3,2,1,0:T(2,128)(2,1)S(1)}, u32[]{:S(2)}, u32[]{:S(2)}) async-start(bf16[16,17,2,128]{3,2,1,0:T(2,128)(2,1)} %states.1), calls=%async_computation | async-start | bytes 278528 | tf_op jit(solution)/shard_map/all_to_all | solution.py:256
  21.3 0.0 copy-start.1
  21.3 0.0 copy-done
  21.3 0.0 copy-done.2
  21.3 0.6 copy-done.1
  22.0 4.9 %within.1 = (f32[512,512]{1,0:T(8,128)S(1)}, bf16[512,512]{1,0:T(8,128)(2,1)S(1)}, f32[1,512]{1,0:T(1,128)S(1)}) custom-call(s32[32]{0:T(128)S(1)} %copy-done.1, bf16[512,512]{1,0:T(8,128)(2,1)} %query_hbm.1, bf16[512,512]{1,0:T(8,128)(2,1)} %key_hbm.3, bf16[512,512]{1,0:T(8,128)(2,1)} %value_hbm.3, f32[4,512]{1,0:T(4,128)S(1)} %bitcast.11, ...), custom_call_target="tpu_custom_call" | custom-call | flops 536870912 | bytes 2359296 | tf_op jit(solution)/shard_map/within/pallas_call | solution.py:257
  26.8 1.3 %all-to-all-done.taken_ref = bf16[16,17,2,128]{3,2,1,0:T(2,128)(2,1)S(1)} async-done(((bf16[16,17,2,128]{3,2,1,0:T(2,128)(2,1)}), bf16[16,17,2,128]{3,2,1,0:T(2,128)(2,1)S(1)}, u32[]{:S(2)}, u32[]{:S(2)}) %all-to-all-start) | async-done | bytes 139296 | tf_op jit(solution)/shard_map/all_to_all | solution.py:256
  28.2 0.2 total.1
  28.4 1.3 %collective-permute-start = (f32[16,2,128]{2,1,0:T(2,128)S(1)}, f32[16,2,128]{2,1,0:T(2,128)S(1)}, u32[]{:S(2)}, u32[]{:S(2)}) collective-permute-start(f32[16,2,128]{2,1,0:T(2,128)S(1)} %total.1), channel_id=1, source_target_pairs={{128,256},{136,264},{144,272},{152,280},{160,288},{168,296},{176,3... | collective-permute-start | bytes 49160 | tf_op jit(solution)/shard_map/ppermute | solution.py:282
  29.7 0.2 prefix.1
  29.9 4.1 %collective-permute-done = f32[16,2,128]{2,1,0:T(2,128)S(1)} collective-permute-done((f32[16,2,128]{2,1,0:T(2,128)S(1)}, f32[16,2,128]{2,1,0:T(2,128)S(1)}, u32[]{:S(2)}, u32[]{:S(2)}) %collective-permute-start) | collective-permute-done | bytes 16416 | tf_op jit(solution)/shard_map/ppermute | solution.py:282
  34.0 16.9 %all_to_all.15 = bf16[16,32,128]{2,1,0:T(8,128)(2,1)S(1)} all-to-all(bf16[16,32,128]{2,1,0:T(8,128)(2,1)S(1)} %enter.1), channel_id=1, replica_groups={{64,72,80,88,96,104,112,120,0,8,16,24,32,40,48,56},{192,200,208,216,224..., dimensions={0} | all-to-all | bytes 262144 | tf_op jit(solution)/shard_map/all_to_all | solution.py:303
  51.0 0.5 finish.1
  51.5 12.8 %all_to_all.16.landed_ref = bf16[8,64,512]{2,1,0:T(8,128)(2,1)S(1)} all-to-all(bf16[8,64,512]{2,1,0:T(8,128)(2,1)S(1)} %finish.1), channel_id=1, replica_groups={{4,5,6,7,0,1,2,3},{12,13,14,15,8,9,10,11},{20,21,22,23,16,17,18,19},{28..., dimensions={0} | all-to-all | bytes 1048576 | tf_op jit(solution)/shard_map/all_to_all | solution.py:314
  64.2 0.8 %place.1 = bf16[64,4096]{1,0:T(8,128)(2,1)} custom-call(bf16[8,64,512]{2,1,0:T(8,128)(2,1)S(1)} %all_to_all.16.landed_ref), custom_call_target="tpu_custom_call" | custom-call | tf_op jit(solution)/shard_map/place/pallas_call | solution.py:317
  (1 shorter events, 0.0 us)
Async XLA Ops:
  2.4 18.9 %copy-start = (f32[512,4]{0,1:T(4,128)S(1)}, f32[512,4]{0,1:T(4,128)}, u32[]{:S(2)}) copy-start(f32[512,4]{0,1:T(4,128)} %param.9) | copy-start | bytes 24580
  2.4 18.9 %copy-start.2 = (f32[512]{0:T(512)S(1)}, f32[512]{0:T(512)}, u32[]{:S(2)}) copy-start(f32[512]{0:T(512)} %param.11) | copy-start | bytes 6148
  2.4 25.7 %all-to-all-start = ((bf16[16,17,2,128]{3,2,1,0:T(2,128)(2,1)}), bf16[16,17,2,128]{3,2,1,0:T(2,128)(2,1)S(1)}, u32[]{:S(2)}, u32[]{:S(2)}) async-start(bf16[16,17,2,128]{3,2,1,0:T(2,128)(2,1)} %states.1), calls=%async_computation | async-start | bytes 278528 | tf_op jit(solution)/shard_map/all_to_all | solution.py:256
  21.3 0.7 %copy-start.1 = (s32[32]{0:T(128)S(1)}, s32[32]{0:T(128)}, u32[]{:S(2)}) copy-start(s32[32]{0:T(128)} %lengths_ref.1) | copy-start | bytes 388
  28.4 5.6 %collective-permute-start = (f32[16,2,128]{2,1,0:T(2,128)S(1)}, f32[16,2,128]{2,1,0:T(2,128)S(1)}, u32[]{:S(2)}, u32[]{:S(2)}) collective-permute-start(f32[16,2,128]{2,1,0:T(2,128)S(1)} %total.1), channel_id=1, source_target_pairs={{128,256},{136,264},{144,272},{152,280},{160,288},{168,296},{176,3... | collective-permute-start | bytes 49160 | tf_op jit(solution)/shard_map/ppermute | solution.py:282

commit v6 on v5

--- a/solution.py
+++ b/solution.py
@@ -12,16 +12,12 @@
 NEVER = -1e30
 PAIR = 2
 CHUNK = 128
-FIRST_Z = 8
-FIRST_SECTION = 4
-
-
-def place(position, count):
-    return (position + FIRST_Z) % count
+ORDER_Z = (8, 7, 6, 5, 4, 3, 2, 1, 0, 15, 14, 13, 12, 11, 10, 9)
+ORDER_SECTION = (5, 4, 7, 6, 1, 0, 3, 2)
 
 
 def in_chain(count):
-    return sorted(range(count), key=lambda position: place(position, count))
+    return sorted(range(count), key=lambda position: ORDER_Z[position])
 
 
 def dot(a, b, contract):
@@ -229,7 +225,7 @@
     heads = log_decay.shape[1]
     dim = width // heads
     holders = lax.axis_size("seq") // 4
-    chains = [[at + place(i, holders) for i in range(holders)] for at in range(0, 4 * holders, holders)]
+    chains = [[at + z for z in ORDER_Z] for at in range(0, 4 * holders, holders)]
     onward = [(holders + i, 2 * holders + i) for i in range(holders)]
     slots = width // holders
     pairs = slots // PAIR
@@ -302,7 +298,7 @@
     )(before.reshape(width, dim), reach.reshape(holders * PAIR, dim), entering.reshape(slots, dim))
     incoming = lax.all_to_all(given, "seq", split_axis=0, concat_axis=0, tiled=True, axis_index_groups=chains)
     count = lax.axis_size("section")
-    sections = [(i + FIRST_SECTION) % count for i in range(count)]
+    sections = list(ORDER_SECTION)
     normed = pl.pallas_call(
         functools.partial(finish_kernel, sections),
         out_shape=jax.ShapeDtypeStruct((count, rows // count, width), BF16),

time: 65.4 us -> 65 us (level)
  the two profiles are of different devices: /device:TPU:20 before, /device:TPU:16 now
where the time goes in v6:
time: 65 us; the launch traced here: 64.5 us
  blocking collectives  29.1 us (45%)
  starting transfers between devices  20.2 us (31%)
  Pallas kernels  9.06 us (14%)
  waiting for transfers between devices  5.45 us (8%)
    all_to_all x1, starting transfers between devices, shards(): lax.all_to_all(states, 'seq', split_axis=0, concat_axis=0, tiled=True, ax...  18.9 us
    all_to_all x1, blocking collectives, shards(): lax.all_to_all(given, 'seq', split_axis=0, concat_axis=0, tiled=True, axi...  16.9 us
    all_to_all x1, blocking collectives, shards(): lax.all_to_all(normed, 'section', split_axis=0, concat_axis=0, tiled=True...  12.1 us
    pallas_call x1, Pallas kernels, shards(): pl.pallas_call(within_kernel, out_shape=(jax.ShapeDtypeStruct((rows, widt...  4.87 us
    ppermute x1, waiting for transfers between devices, shards(): entering = lax.ppermute(total, 'seq', onward)  4.14 us
    pallas_call x1, Pallas kernels, shards(): pl.pallas_call(state_kernel, out_shape=jax.ShapeDtypeStruct((holders, pai...  2.4 us
    all_to_all x1, waiting for transfers between devices, shards(): lax.all_to_all(states, 'seq', split_axis=0, concat_axis=0, tiled=True, ax...  1.32 us
  transfers between devices with their start and end apart: 2, of which 2 were waited for; matrix products, arithmetic and copies ran while one was open for 0% of the time, Pallas kernels for 8%

profile of v6, /device:TPU:16, one launch (start us, length us, event | category | flops | bytes accessed | tf_op | source)
XLA Modules:
  0.0 64.5 jit_solution(8130432295732974127)
XLA Ops:
  0.0 2.4 %states.1 = bf16[16,17,2,128]{3,2,1,0:T(2,128)(2,1)} custom-call(s32[32]{0:T(128)} %lengths_ref.1, bf16[512,512]{1,0:T(8,128)(2,1)} %key_hbm.3, bf16[512,512]{1,0:T(8,128)(2,1)} %value_hbm.3, f32[4,512]{1,0:T(4,128)} %bitcast.10), custom_call_target="tpu_custom_call" | custom-call | tf_op jit(solution)/shard_map/states/pallas_call | solution.py:237
  2.4 0.0 copy-start
  2.4 0.0 copy-start.2
  2.4 18.9 %all-to-all-start = ((bf16[16,17,2,128]{3,2,1,0:T(2,128)(2,1)}), bf16[16,17,2,128]{3,2,1,0:T(2,128)(2,1)S(1)}, u32[]{:S(2)}, u32[]{:S(2)}) async-start(bf16[16,17,2,128]{3,2,1,0:T(2,128)(2,1)} %states.1), calls=%async_computation | async-start | bytes 278528 | tf_op jit(solution)/shard_map/all_to_all | solution.py:252
  21.3 0.0 copy-start.1
  21.3 0.0 copy-done
  21.3 0.0 copy-done.2
  21.3 0.6 copy-done.1
  22.0 4.9 %within.1 = (f32[512,512]{1,0:T(8,128)S(1)}, bf16[512,512]{1,0:T(8,128)(2,1)S(1)}, f32[1,512]{1,0:T(1,128)S(1)}) custom-call(s32[32]{0:T(128)S(1)} %copy-done.1, bf16[512,512]{1,0:T(8,128)(2,1)} %query_hbm.1, bf16[512,512]{1,0:T(8,128)(2,1)} %key_hbm.3, bf16[512,512]{1,0:T(8,128)(2,1)} %value_hbm.3, f32[4,512]{1,0:T(4,128)S(1)} %bitcast.11, ...), custom_call_target="tpu_custom_call" | custom-call | flops 536870912 | bytes 2359296 | tf_op jit(solution)/shard_map/within/pallas_call | solution.py:253
  26.8 1.3 %all-to-all-done.taken_ref = bf16[16,17,2,128]{3,2,1,0:T(2,128)(2,1)S(1)} async-done(((bf16[16,17,2,128]{3,2,1,0:T(2,128)(2,1)}), bf16[16,17,2,128]{3,2,1,0:T(2,128)(2,1)S(1)}, u32[]{:S(2)}, u32[]{:S(2)}) %all-to-all-start) | async-done | bytes 139296 | tf_op jit(solution)/shard_map/all_to_all | solution.py:252
  28.2 0.2 total.1
  28.4 1.3 %collective-permute-start = (f32[16,2,128]{2,1,0:T(2,128)S(1)}, f32[16,2,128]{2,1,0:T(2,128)S(1)}, u32[]{:S(2)}, u32[]{:S(2)}) collective-permute-start(f32[16,2,128]{2,1,0:T(2,128)S(1)} %total.1), channel_id=1, source_target_pairs={{128,256},{136,264},{144,272},{152,280},{160,288},{168,296},{176,3... | collective-permute-start | bytes 49160 | tf_op jit(solution)/shard_map/ppermute | solution.py:278
  29.7 0.2 prefix.1
  29.8 4.1 %collective-permute-done = f32[16,2,128]{2,1,0:T(2,128)S(1)} collective-permute-done((f32[16,2,128]{2,1,0:T(2,128)S(1)}, f32[16,2,128]{2,1,0:T(2,128)S(1)}, u32[]{:S(2)}, u32[]{:S(2)}) %collective-permute-start) | collective-permute-done | bytes 16416 | tf_op jit(solution)/shard_map/ppermute | solution.py:278
  34.0 16.9 %all_to_all.15 = bf16[16,32,128]{2,1,0:T(8,128)(2,1)S(1)} all-to-all(bf16[16,32,128]{2,1,0:T(8,128)(2,1)S(1)} %enter.1), channel_id=1, replica_groups={{64,56,48,40,32,24,16,8,0,120,112,104,96,88,80,72},{192,184,176,168,160..., dimensions={0} | all-to-all | bytes 262144 | tf_op jit(solution)/shard_map/all_to_all | solution.py:299
  51.0 0.5 finish.1
  51.5 12.1 %all_to_all.16.landed_ref = bf16[8,64,512]{2,1,0:T(8,128)(2,1)S(1)} all-to-all(bf16[8,64,512]{2,1,0:T(8,128)(2,1)S(1)} %finish.1), channel_id=1, replica_groups={{5,4,7,6,1,0,3,2},{13,12,15,14,9,8,11,10},{21,20,23,22,17,16,19,18},{29..., dimensions={0} | all-to-all | bytes 1048576 | tf_op jit(solution)/shard_map/all_to_all | solution.py:310
  63.6 0.8 %place.1 = bf16[64,4096]{1,0:T(8,128)(2,1)} custom-call(bf16[8,64,512]{2,1,0:T(8,128)(2,1)S(1)} %all_to_all.16.landed_ref), custom_call_target="tpu_custom_call" | custom-call | tf_op jit(solution)/shard_map/place/pallas_call | solution.py:313
  (1 shorter events, 0.0 us)
Async XLA Ops:
  2.4 18.9 %copy-start = (f32[512,4]{0,1:T(4,128)S(1)}, f32[512,4]{0,1:T(4,128)}, u32[]{:S(2)}) copy-start(f32[512,4]{0,1:T(4,128)} %param.9) | copy-start | bytes 24580
  2.4 18.9 %copy-start.2 = (f32[512]{0:T(512)S(1)}, f32[512]{0:T(512)}, u32[]{:S(2)}) copy-start(f32[512]{0:T(512)} %param.11) | copy-start | bytes 6148
  2.4 25.7 %all-to-all-start = ((bf16[16,17,2,128]{3,2,1,0:T(2,128)(2,1)}), bf16[16,17,2,128]{3,2,1,0:T(2,128)(2,1)S(1)}, u32[]{:S(2)}, u32[]{:S(2)}) async-start(bf16[16,17,2,128]{3,2,1,0:T(2,128)(2,1)} %states.1), calls=%async_computation | async-start | bytes 278528 | tf_op jit(solution)/shard_map/all_to_all | solution.py:252
  21.3 0.7 %copy-start.1 = (s32[32]{0:T(128)S(1)}, s32[32]{0:T(128)}, u32[]{:S(2)}) copy-start(s32[32]{0:T(128)} %lengths_ref.1) | copy-start | bytes 388
  28.4 5.6 %collective-permute-start = (f32[16,2,128]{2,1,0:T(2,128)S(1)}, f32[16,2,128]{2,1,0:T(2,128)S(1)}, u32[]{:S(2)}, u32[]{:S(2)}) collective-permute-start(f32[16,2,128]{2,1,0:T(2,128)S(1)} %total.1), channel_id=1, source_target_pairs={{128,256},{136,264},{144,272},{152,280},{160,288},{168,296},{176,3... | collective-permute-start | bytes 49160 | tf_op jit(solution)/shard_map/ppermute | solution.py:278

commit v7 on v6

--- a/solution.py
+++ b/solution.py
@@ -163,7 +163,7 @@
     carry = jnp.zeros(total_ref.shape, F32)
     for block in in_chain(blocks):
         carry = taken_ref[block, 0:pairs].astype(F32) + kept_of(taken_ref, block) * carry
-    total_ref[...] = carry
+    total_ref[...] = carry.astype(BF16)
 
 
 def prefix_kernel(taken_ref, before_ref, reach_ref):
@@ -180,7 +180,7 @@
 
 def enter_kernel(before_ref, reach_ref, entering_ref, out_ref):
     slots = entering_ref.shape[0]
-    entering = entering_ref[...]
+    entering = entering_ref[...].astype(F32)
     for block in range(out_ref.shape[0]):
         at = pl.ds(block * slots, slots)
         reach = reach_ref[block * PAIR : block * PAIR + 1, :]
@@ -269,7 +269,7 @@
     taken, within, decayed, gain = lax.optimization_barrier((taken, within, decayed, gain))
     total = pl.pallas_call(
         total_kernel,
-        out_shape=jax.ShapeDtypeStruct((pairs, PAIR, dim), F32),
+        out_shape=jax.ShapeDtypeStruct((pairs, PAIR, dim), BF16),
         in_specs=[vmem],
         out_specs=vmem,
         compiler_params=params(),

time: 65 us -> 64.9 us (level)
  no operation moved by 1% of the time
where the time goes in v7:
time: 64.9 us; the launch traced here: 64.4 us
  blocking collectives  29.1 us (45%)
  starting transfers between devices  20.2 us (31%)
  Pallas kernels  9.06 us (14%)
  waiting for transfers between devices  5.36 us (8%)
    all_to_all x1, starting transfers between devices, shards(): lax.all_to_all(states, 'seq', split_axis=0, concat_axis=0, tiled=True, ax...  18.9 us
    all_to_all x1, blocking collectives, shards(): lax.all_to_all(given, 'seq', split_axis=0, concat_axis=0, tiled=True, axi...  16.9 us
    all_to_all x1, blocking collectives, shards(): lax.all_to_all(normed, 'section', split_axis=0, concat_axis=0, tiled=True...  12.1 us
    pallas_call x1, Pallas kernels, shards(): pl.pallas_call(within_kernel, out_shape=(jax.ShapeDtypeStruct((rows, widt...  4.87 us
    ppermute x1, waiting for transfers between devices, shards(): entering = lax.ppermute(total, 'seq', onward)  4.05 us
    pallas_call x1, Pallas kernels, shards(): pl.pallas_call(state_kernel, out_shape=jax.ShapeDtypeStruct((holders, pai...  2.4 us
    all_to_all x1, waiting for transfers between devices, shards(): lax.all_to_all(states, 'seq', split_axis=0, concat_axis=0, tiled=True, ax...  1.32 us
  transfers between devices with their start and end apart: 2, of which 2 were waited for; matrix products, arithmetic and copies ran while one was open for 0% of the time, Pallas kernels for 8%

profile of v7, /device:TPU:16, one launch (start us, length us, event | category | flops | bytes accessed | tf_op | source)
XLA Modules:
  0.0 64.4 jit_solution(140500535462013045)
XLA Ops:
  0.0 2.4 %states.1 = bf16[16,17,2,128]{3,2,1,0:T(2,128)(2,1)} custom-call(s32[32]{0:T(128)} %lengths_ref.1, bf16[512,512]{1,0:T(8,128)(2,1)} %key_hbm.3, bf16[512,512]{1,0:T(8,128)(2,1)} %value_hbm.3, f32[4,512]{1,0:T(4,128)} %bitcast.9), custom_call_target="tpu_custom_call" | custom-call | tf_op jit(solution)/shard_map/states/pallas_call | solution.py:237
  2.4 0.0 copy-start
  2.4 0.0 copy-start.2
  2.4 18.9 %all-to-all-start = ((bf16[16,17,2,128]{3,2,1,0:T(2,128)(2,1)}), bf16[16,17,2,128]{3,2,1,0:T(2,128)(2,1)S(1)}, u32[]{:S(2)}, u32[]{:S(2)}) async-start(bf16[16,17,2,128]{3,2,1,0:T(2,128)(2,1)} %states.1), calls=%async_computation | async-start | bytes 278528 | tf_op jit(solution)/shard_map/all_to_all | solution.py:252
  21.3 0.0 copy-start.1
  21.3 0.0 copy-done
  21.3 0.0 copy-done.2
  21.3 0.6 copy-done.1
  22.0 4.9 %within.1 = (f32[512,512]{1,0:T(8,128)S(1)}, bf16[512,512]{1,0:T(8,128)(2,1)S(1)}, f32[1,512]{1,0:T(1,128)S(1)}) custom-call(s32[32]{0:T(128)S(1)} %copy-done.1, bf16[512,512]{1,0:T(8,128)(2,1)} %query_hbm.1, bf16[512,512]{1,0:T(8,128)(2,1)} %key_hbm.3, bf16[512,512]{1,0:T(8,128)(2,1)} %value_hbm.3, f32[4,512]{1,0:T(4,128)S(1)} %bitcast.10, ...), custom_call_target="tpu_custom_call" | custom-call | flops 536870912 | bytes 2359296 | tf_op jit(solution)/shard_map/within/pallas_call | solution.py:253
  26.8 1.3 %all-to-all-done.taken_ref = bf16[16,17,2,128]{3,2,1,0:T(2,128)(2,1)S(1)} async-done(((bf16[16,17,2,128]{3,2,1,0:T(2,128)(2,1)}), bf16[16,17,2,128]{3,2,1,0:T(2,128)(2,1)S(1)}, u32[]{:S(2)}, u32[]{:S(2)}) %all-to-all-start) | async-done | bytes 139296 | tf_op jit(solution)/shard_map/all_to_all | solution.py:252
  28.2 0.2 total.1
  28.4 1.3 %collective-permute-start = (bf16[16,2,128]{2,1,0:T(2,128)(2,1)S(1)}, bf16[16,2,128]{2,1,0:T(2,128)(2,1)S(1)}, u32[]{:S(2)}, u32[]{:S(2)}) collective-permute-start(bf16[16,2,128]{2,1,0:T(2,128)(2,1)S(1)} %total.1), channel_id=1, source_target_pairs={{128,256},{136,264},{144,272},{152,280},{160,288},{168,296},{176,3... | collective-permute-start | bytes 24584 | tf_op jit(solution)/shard_map/ppermute | solution.py:278
  29.7 0.2 prefix.1
  29.9 4.0 %collective-permute-done = bf16[16,2,128]{2,1,0:T(2,128)(2,1)S(1)} collective-permute-done((bf16[16,2,128]{2,1,0:T(2,128)(2,1)S(1)}, bf16[16,2,128]{2,1,0:T(2,128)(2,1)S(1)}, u32[]{:S(2)}, u32[]{:S(2)}) %collective-permute-start) | collective-permute-done | bytes 8224 | tf_op jit(solution)/shard_map/ppermute | solution.py:278
  33.9 16.9 %all_to_all.15 = bf16[16,32,128]{2,1,0:T(8,128)(2,1)S(1)} all-to-all(bf16[16,32,128]{2,1,0:T(8,128)(2,1)S(1)} %enter.1), channel_id=1, replica_groups={{64,56,48,40,32,24,16,8,0,120,112,104,96,88,80,72},{192,184,176,168,160..., dimensions={0} | all-to-all | bytes 262144 | tf_op jit(solution)/shard_map/all_to_all | solution.py:299
  50.9 0.5 finish.1
  51.4 12.1 %all_to_all.16.landed_ref = bf16[8,64,512]{2,1,0:T(8,128)(2,1)S(1)} all-to-all(bf16[8,64,512]{2,1,0:T(8,128)(2,1)S(1)} %finish.1), channel_id=1, replica_groups={{5,4,7,6,1,0,3,2},{13,12,15,14,9,8,11,10},{21,20,23,22,17,16,19,18},{29..., dimensions={0} | all-to-all | bytes 1048576 | tf_op jit(solution)/shard_map/all_to_all | solution.py:310
  63.5 0.8 %place.1 = bf16[64,4096]{1,0:T(8,128)(2,1)} custom-call(bf16[8,64,512]{2,1,0:T(8,128)(2,1)S(1)} %all_to_all.16.landed_ref), custom_call_target="tpu_custom_call" | custom-call | tf_op jit(solution)/shard_map/place/pallas_call | solution.py:313
  (1 shorter events, 0.0 us)
Async XLA Ops:
  2.4 18.9 %copy-start = (f32[512,4]{0,1:T(4,128)S(1)}, f32[512,4]{0,1:T(4,128)}, u32[]{:S(2)}) copy-start(f32[512,4]{0,1:T(4,128)} %param.9) | copy-start | bytes 24580
  2.4 18.9 %copy-start.2 = (f32[512]{0:T(512)S(1)}, f32[512]{0:T(512)}, u32[]{:S(2)}) copy-start(f32[512]{0:T(512)} %param.11) | copy-start | bytes 6148
  2.4 25.7 %all-to-all-start = ((bf16[16,17,2,128]{3,2,1,0:T(2,128)(2,1)}), bf16[16,17,2,128]{3,2,1,0:T(2,128)(2,1)S(1)}, u32[]{:S(2)}, u32[]{:S(2)}) async-start(bf16[16,17,2,128]{3,2,1,0:T(2,128)(2,1)} %states.1), calls=%async_computation | async-start | bytes 278528 | tf_op jit(solution)/shard_map/all_to_all | solution.py:252
  21.3 0.7 %copy-start.1 = (s32[32]{0:T(128)S(1)}, s32[32]{0:T(128)}, u32[]{:S(2)}) copy-start(s32[32]{0:T(128)} %lengths_ref.1) | copy-start | bytes 388
  28.4 5.5 %collective-permute-start = (bf16[16,2,128]{2,1,0:T(2,128)(2,1)S(1)}, bf16[16,2,128]{2,1,0:T(2,128)(2,1)S(1)}, u32[]{:S(2)}, u32[]{:S(2)}) collective-permute-start(bf16[16,2,128]{2,1,0:T(2,128)(2,1)S(1)} %total.1), channel_id=1, source_target_pairs={{128,256},{136,264},{144,272},{152,280},{160,288},{168,296},{176,3... | collective-permute-start | bytes 24584 | tf_op jit(solution)/shard_map/ppermute | solution.py:278
